TPU v7x, 32 devices: a whole 2x2x4 slice. The times are simulated.
32 devices in a mesh: layer: 4 (over z), row: 2 (over x), col: 4 (over y, core).
Axes of the slice: x: 2, y: 2, z: 4, core: 2. Of those that a mesh axis runs over, the one named last changes fastest.
Arguments:
- cost_vector: float32 [8, 1024, 512], P('layer', 'row', 'col'), may hold values from -12 to 12
- metal_density: float32 [8, 1024, 512], P('layer', 'row', 'col'), may hold values from 0 to 0.5
- cap_class: int32 [8, 1024, 512], P('layer', 'row', 'col'), may hold values from 0 to 7
- blocked_mask: int32 [8, 1024, 512], P('layer', 'row', 'col'), may hold values 0 or 1
- fill_start: float32 [8, 1024, 512], P('layer', 'row', 'col'), may hold values from 0 to 1
- window_dual: float32 [8, 1024, 512], P('layer', 'row', 'col'), may hold values from -4 to 4
- layer_dual: float32 [8, 1024, 512], P('layer', 'row', 'col'), may hold values from -4 to 4
Outputs:
- fill_level: float32 [8, 1024, 512], P('layer', 'row', 'col')
- window_price: float32 [8, 1024, 512], P('layer', 'row', 'col')
- layer_price: float32 [8, 1024, 512], P('layer', 'row', 'col')
- primal_weight: float32 [], replicated
All inputs are finite; a program needn't handle non-finite values. No bound on the sum of `blocked_mask` on one device may be relied on, other than what follows from the above.
Results may differ from a plain program's by a relative error of at most 0.00011.
Values sent between devices are 32-bit elements; how exact they have to be, the bound alone decides.
A program may use at most 64 MiB of HBM per device.

v0:
```python
import functools

import jax
import jax.numpy as jnp
from jax import lax
from jax.experimental import pallas as pl
from jax.experimental.pallas import tpu as pltpu
from jax.sharding import PartitionSpec as P

WIN = 50
CAP_LEVELS = 8
ITERS = 3

step_eta = 0.4
low_density = 0.35
high_density = 0.65
layer_gap = 0.15
tiny_term = 1e-06

HALF = WIN // 2
HALO = -(-HALF // 16) * 16
TILE = 128
MESH = pl.DeviceIdType.MESH
DIRS = ((-1, 0), (1, 0), (0, -1), (0, 1), (-1, -1), (-1, 1), (1, -1), (1, 1))
F32 = jnp.float32
BF16 = jnp.bfloat16
NT = (((1,), (1,)), ((), ()))
NN = (((1,), (0,)), ((), ()))


def split(value):
    high = value.astype(BF16)
    low = (value - high.astype(F32)).astype(BF16)
    return high, low


def dot(left, right, dims=NN):
    return lax.dot_general(left, right, dims, preferred_element_type=F32)


def iota(shape, dim):
    return lax.broadcasted_iota(jnp.int32, shape, dim)


def window(offset, start):
    return jnp.where((offset >= start) & (offset < start + WIN), 1.0, 0.0).astype(BF16)


def kernel(
    sizes, cost_in, dens_in, capc_in, blocked_in, x_in, y_in, z_in,
    x, y_out, z, weight_out,
    cost, dens, capc, blocked,
    ext_u, ext_y, et_u, et_y, ht_u, ht_y, above, below, zlow, cap, grad,
    band_r, band_h, band_c, pick, slots,
    load_sem, send_sem, recv_sem, first_sem, zsend, zrecv, sum_sem,
):
    nl, nr, nc = sizes
    layers, rows, cols = x_in.shape
    ndev = nl * nr * nc
    il, ir, ic = lax.axis_index("layer"), lax.axis_index("row"), lax.axis_index("col")
    me = (il * nr + ir) * nc + ic
    tiles = rows // TILE
    order = list(dict.fromkeys((0, tiles - 1, *range(tiles))))
    inverse_area = 1.0 / (WIN * WIN)
    own = pl.ds(HALO, rows)

    pairs = (
        (y_in, ext_y.at[:, own, :]), (x_in, x), (z_in, z), (cost_in, cost), (capc_in, capc),
        (blocked_in, blocked), (dens_in, dens),
    )
    loads = [pltpu.make_async_copy(a, b, load_sem.at[n]) for n, (a, b) in enumerate(pairs)]
    for load in loads:
        load.start()

    for ref in (ext_u, ext_y):
        ref[:, :HALO, :] = jnp.zeros((layers, HALO, cols), F32)
        ref[:, HALO + rows :, :] = jnp.zeros((layers, HALO, cols), F32)
    for ref in (ht_u, ht_y, above, below, zlow):
        ref[...] = jnp.zeros(ref.shape, F32)

    barrier = pltpu.get_barrier_semaphore()

    def others(act):
        def one(i, _):
            pl.when(i != me)(lambda: act((i // (nr * nc), (i // nc) % nr, i % nc)))
            return 0

        lax.fori_loop(0, ndev, one, 0, unroll=ndev <= 32)

    def greet(device):
        pl.semaphore_signal(barrier, inc=1, device_id=device, device_id_type=MESH)

    others(greet)

    keep_top = jnp.where(il < nl - 1, 1.0, 0.0).astype(F32)
    keep_low = jnp.where(il > 0, 1.0, 0.0).astype(F32)
    for which, start in ((0, -HALF), (1, 1 - HALF)):
        shape = (TILE, TILE + 2 * HALO)
        band_r[which] = window(iota(shape, 1) - HALO - iota(shape, 0), start)
        shape = (TILE, 3 * TILE)
        band_h[which] = window(iota(shape, 1) - TILE - iota(shape, 0), start)
        shape = (cols, cols)
        inner = window(iota(shape, 0) - iota(shape, 1), start)
        shape = (2 * HALO, cols)
        k = iota(shape, 0)
        place = jnp.where(k < HALO, k - HALO, k - HALO + cols)
        outer = window(place - iota(shape, 1), start)
        blank = jnp.zeros(shape, BF16)
        half = cols + layers * 2 * HALO
        for l in range(layers):
            for base in (0, half):
                band_c[which, l, base : base + cols] = inner
                for m in range(layers):
                    at = base + cols + m * 2 * HALO
                    band_c[which, l, at : at + 2 * HALO] = outer if m == l else blank
    shape = (2 * HALO, cols)
    k = iota(shape, 0)
    place = jnp.where(k < HALO, k, k - 2 * HALO + cols)
    pick[...] = jnp.where(place == iota(shape, 1), 1.0, 0.0).astype(BF16)

    def span(t, base=0):
        return pl.ds(t * TILE + base, TILE)

    def put_edges(et, l, t, value):
        et[l, :, span(t)] = dot(pick[...], value.astype(BF16), NT)

    loads[0].wait()
    for t in range(tiles):
        for l in range(layers):
            put_edges(et_y, l, t, ext_y[l, span(t, HALO), :])

    pl.semaphore_wait(barrier, ndev - 1)

    def copies(field):
        ext, et, ht = ((ext_u, et_u, ht_u), (ext_y, et_y, ht_y))[field]
        result = []
        for d, (dr, dc) in enumerate(DIRS):
            if dc == 0:
                src = ext.at[:, pl.ds(HALO if dr < 0 else rows, HALO), :]
                dst = ext.at[:, pl.ds(HALO + rows if dr < 0 else 0, HALO), :]
            else:
                from_rows = pl.ds(0 if dc < 0 else HALO, HALO)
                to_rows = pl.ds(HALO if dc < 0 else 0, HALO)
                if dr == 0:
                    src, dst = et.at[:, from_rows, :], ht.at[:, to_rows, pl.ds(TILE, rows)]
                elif dr < 0:
                    src = et.at[:, from_rows, pl.ds(0, TILE)]
                    dst = ht.at[:, to_rows, pl.ds(TILE + rows, TILE)]
                else:
                    src = et.at[:, from_rows, pl.ds(rows - TILE, TILE)]
                    dst = ht.at[:, to_rows, pl.ds(0, TILE)]
            to, frm = [], []
            if dr < 0:
                to.append(ir > 0)
                frm.append(ir < nr - 1)
            if dr > 0:
                to.append(ir < nr - 1)
                frm.append(ir > 0)
            if dc < 0:
                to.append(ic > 0)
                frm.append(ic < nc - 1)
            if dc > 0:
                to.append(ic < nc - 1)
                frm.append(ic > 0)
            copy = pltpu.make_async_remote_copy(
                src_ref=src, dst_ref=dst, send_sem=send_sem.at[field, d],
                recv_sem=recv_sem.at[field, d],
                device_id=(il, ir + dr, ic + dc), device_id_type=MESH,
            )
            result.append(
                (copy, functools.reduce(jnp.logical_and, to), functools.reduce(jnp.logical_and, frm))
            )
        return result

    halo_copies = (copies(0), copies(1))

    def begin(field, which):
        for d in which:
            copy, to, _ = halo_copies[field][d]
            pl.when(to)(copy.start)

    def finish(field):
        for copy, to, frm in halo_copies[field]:
            pl.when(frm)(copy.wait_recv)
            pl.when(to)(copy.wait_send)

    has_above, has_below = il < nl - 1, il > 0
    EDGE, SIDE = (4, 5, 6, 7, 0, 1), (2, 3)
    begin(1, EDGE + SIDE)
    first_up = pltpu.make_async_remote_copy(
        src_ref=z_in.at[layers - 1], dst_ref=zlow, send_sem=first_sem.at[0],
        recv_sem=first_sem.at[1], device_id=(il + 1, ir, ic), device_id_type=MESH,
    )
    pl.when(has_above)(first_up.start)

    def up(t):
        return pltpu.make_async_remote_copy(
            src_ref=ext_u.at[layers - 1, span(t, HALO), :], dst_ref=below.at[span(t), :],
            send_sem=zsend.at[0, t], recv_sem=zrecv.at[0, t],
            device_id=(il + 1, ir, ic), device_id_type=MESH,
        )

    def down(t):
        return pltpu.make_async_remote_copy(
            src_ref=ext_u.at[0, span(t, HALO), :], dst_ref=above.at[span(t), :],
            send_sem=zsend.at[1, t], recv_sem=zrecv.at[1, t],
            device_id=(il - 1, ir, ic), device_id_type=MESH,
        )

    def box(ext, ht, which, t):
        tall = pl.ds(t * TILE, TILE + 2 * HALO)
        wide = jnp.concatenate([ext[l, tall, :].astype(BF16) for l in range(layers)], axis=1)
        mid = dot(band_r[which], wide)
        halo = ht[:, :, t * TILE : (t + 3) * TILE].reshape(layers * 2 * HALO, 3 * TILE)
        side = dot(band_h[which], halo.astype(BF16), NT)
        result = []
        for l in range(layers):
            row = jnp.concatenate([mid[:, l * cols : (l + 1) * cols], side], axis=1)
            result.append(dot(jnp.concatenate(split(row), axis=1), band_c[which, l]))
        return result

    everywhere = [(l, t, (l, span(t), slice(None))) for t in order for l in range(layers)]
    for n in range(1, 7):
        loads[n].wait()
    z[layers - 1] = z[layers - 1] * keep_top
    for l, t, at in everywhere:
        level = (capc[at] + 1).astype(F32) * (1.0 / CAP_LEVELS)
        cap[at] = jnp.where(blocked[at] == 1, 0.0, level)

    def fold(value):
        return jnp.sum((value * value).reshape(TILE // 8, 8, cols), axis=0)

    def sums_begin(step, primal_sum, dual_sum):
        slots[step, pl.ds(me, 1)] = jnp.concatenate(
            [jnp.sum(primal_sum, axis=0, keepdims=True), jnp.sum(dual_sum, axis=0, keepdims=True)],
            axis=0,
        )[None]

        def send(device):
            pltpu.make_async_remote_copy(
                src_ref=slots.at[step, me], dst_ref=slots.at[step, me],
                send_sem=sum_sem.at[0, step], recv_sem=sum_sem.at[1, step],
                device_id=device, device_id_type=MESH,
            ).start()

        others(send)

    def sums_end(step, weight):
        some = slots.at[step, pl.ds(0, ndev - 1)]
        pltpu.make_async_copy(some, some, sum_sem.at[1, step]).wait()
        pltpu.make_async_copy(some, some, sum_sem.at[0, step]).wait()
        both = jnp.sum(slots[step], axis=0)
        primal = jnp.sum(both[0:1], axis=1, keepdims=True)
        dual = jnp.sum(both[1:2], axis=1, keepdims=True)
        ratio = jnp.broadcast_to((dual + tiny_term) / (primal + tiny_term), (1, cols))
        return jnp.sqrt(weight) * jnp.sqrt(jnp.sqrt(ratio))

    weight = jnp.ones((1, cols), F32)
    for step in range(ITERS):
        last = step == ITERS - 1
        if step == 0:
            pl.when(has_below)(first_up.wait_recv)
            pl.when(has_above)(first_up.wait_send)
        finish(1)
        for t in order:
            for l, area in enumerate(box(ext_y, ht_y, 1, t)):
                at = (l, span(t), slice(None))
                earlier = zlow[span(t), :] if l == 0 else z[l - 1, span(t), :]
                grad[at] = cost[at] + area * inverse_area + (z[at] - earlier)
        if step > 0:
            weight = sums_end(step - 1, weight)
        tau = step_eta / weight
        sigma = step_eta * weight
        sigma_inverse = 1.0 / sigma

        primal_sum = jnp.zeros((8, cols), F32)
        for l, t, at in everywhere:
            old = x[at]
            new = jnp.minimum(jnp.maximum(old - tau * grad[at], 0.0), cap[at])
            moved = new - old
            x[at] = new
            primal_sum = primal_sum + fold(moved)
            value = new + moved + dens[at]
            ext_u[l, span(t, HALO), :] = value
            put_edges(et_u, l, t, value)
            if l == layers - 1:
                if not last:
                    pl.when(has_above)(up(t).start)
                pl.when(has_below)(down(t).start)
                if t == order[min(1, tiles - 1)]:
                    begin(0, EDGE)
        begin(0, SIDE)
        finish(0)

        dual_sum = jnp.zeros((8, cols), F32)
        areas = {}
        for l, t, at in everywhere:
            if l == 0:
                areas = box(ext_u, ht_u, 0, t)
            old = ext_y[l, span(t, HALO), :]
            term = old * sigma_inverse + areas[l] * inverse_area
            capped = jnp.minimum(term, high_density)
            clipped = jnp.where(blocked[at] == 0, jnp.maximum(capped, low_density), capped)
            new = sigma * (term - clipped)
            dual_sum = dual_sum + fold(new - old)
            if last:
                y_out[at] = new
            else:
                ext_y[l, span(t, HALO), :] = new
                put_edges(et_y, l, t, new)
                if l == layers - 1 and t == order[min(1, tiles - 1)]:
                    begin(1, EDGE)
        if not last:
            begin(1, SIDE)

        def update(old, here, later, keep):
            term = old * sigma_inverse + keep * (here - later)
            return sigma * (term - jnp.clip(term, -layer_gap, layer_gap)) * keep

        for t in order:
            pl.when(has_above)(down(t).wait_recv)
            pl.when(has_below)(down(t).wait_send)
            if not last:
                pl.when(has_below)(up(t).wait_recv)
                pl.when(has_above)(up(t).wait_send)
            levels = [ext_u[l, span(t, HALO), :] for l in range(layers)] + [above[span(t), :]]
            for l in range(layers):
                at = (l, span(t), slice(None))
                old = z[at]
                new = update(old, levels[l], levels[l + 1], keep_top if l == layers - 1 else 1.0)
                z[at] = new
                dual_sum = dual_sum + fold(new - old)
            if not last:
                zlow[span(t), :] = update(zlow[span(t), :], below[span(t), :], levels[0], keep_low)
        sums_begin(step, primal_sum, dual_sum)

    weight_out[...] = sums_end(ITERS - 1, weight)


def local(sizes, *args):
    layers, rows, cols = args[0].shape
    ndev = sizes[0] * sizes[1] * sizes[2]
    tiles = rows // TILE
    whole = jax.ShapeDtypeStruct((layers, rows, cols), F32)
    vmem = pl.BlockSpec(memory_space=pltpu.VMEM)
    anywhere = pl.BlockSpec(memory_space=pl.ANY)
    full = pltpu.VMEM((layers, rows, cols), F32)
    full_int = pltpu.VMEM((layers, rows, cols), jnp.int32)
    line = pltpu.VMEM((1, cols), F32)
    ext = pltpu.VMEM((layers, rows + 2 * HALO, cols), F32)
    et = pltpu.VMEM((layers, 2 * HALO, rows), F32)
    ht = pltpu.VMEM((layers, 2 * HALO, rows + 2 * TILE), F32)
    plane = pltpu.VMEM((rows, cols), F32)
    x, y, z, weight = pl.pallas_call(
        functools.partial(kernel, sizes),
        out_shape=(full, full, full, line),
        in_specs=[anywhere] * 7,
        out_specs=(vmem,) * 4,
        scratch_shapes=[
            full, full, full_int, full_int,
            ext, ext, et, et, ht, ht, plane, plane, plane, full, full,
            pltpu.VMEM((2, TILE, TILE + 2 * HALO), BF16),
            pltpu.VMEM((2, TILE, 3 * TILE), BF16),
            pltpu.VMEM((2, layers, 2 * (cols + layers * 2 * HALO), cols), BF16),
            pltpu.VMEM((2 * HALO, cols), BF16),
            pltpu.VMEM((ITERS, ndev, 2, cols), F32),
            pltpu.SemaphoreType.DMA((7,)),
            pltpu.SemaphoreType.DMA((2, 8)),
            pltpu.SemaphoreType.DMA((2, 8)),
            pltpu.SemaphoreType.DMA((2,)),
            pltpu.SemaphoreType.DMA((2, tiles)),
            pltpu.SemaphoreType.DMA((2, tiles)),
            pltpu.SemaphoreType.DMA((2, ITERS)),
        ],
        compiler_params=pltpu.CompilerParams(collective_id=0, has_side_effects=True),
        name="fill_steps",
    )(*args)
    return x, y, z, weight[0, 0]


def solution(mesh):
    sizes = tuple(mesh.shape[axis] for axis in ("layer", "row", "col"))
    spec = P("layer", "row", "col")
    return jax.shard_map(
        functools.partial(local, sizes),
        mesh=mesh,
        in_specs=(spec,) * 7,
        out_specs=(spec, spec, spec, P()),
        check_vma=False,
    )
```

profile of v0, /device:TPU:0, one launch (start us, length us, event | category | flops | bytes accessed | tf_op | source)
XLA Modules:
  0.0 56.1 jit_solution(1745573783401668142)
XLA Ops:
  0.6 51.9 %fill_steps.1 = (f32[2,512,128]{2,1,0:T(8,128)S(1)}, f32[2,512,128]{2,1,0:T(8,128)S(1)}, f32[2,512,128]{2,1,0:T(8,128)S(1)}, f32[1,128]{1,0:T(1,128)S(1)}) custom-call(f32[2,512,128]{2,1,0:T(8,128)} %cost_in.1, f32[2,512,128]{2,1,0:T(8,128)} %dens_in.1, s32[2,512,128]{2,1,0:T(8,128)} %capc_in.1, s32[2,512,128]{2,1,0:T(8,128)} %blocked_in.1, ...), custom_call_target="tpu_custom_call" | custom-call | tf_op jit(solution)/shard_map/fill_steps/pallas_call | solution.py:354
  52.6 0.8 %copy.15 = f32[2,512,128]{2,1,0:T(8,128)} copy(f32[2,512,128]{2,1,0:T(8,128)S(1)} %get-tuple-element.12) | data formatting | bytes 1048576
  53.4 0.8 %copy.16 = f32[2,512,128]{2,1,0:T(8,128)} copy(f32[2,512,128]{2,1,0:T(8,128)S(1)} %get-tuple-element.13) | data formatting | bytes 1048576
  54.1 0.8 %copy.17 = f32[2,512,128]{2,1,0:T(8,128)} copy(f32[2,512,128]{2,1,0:T(8,128)S(1)} %get-tuple-element.14) | data formatting | bytes 1048576
where the time goes:
time: 56.3 us; the launch traced here: 56.1 us
  Pallas kernels  51.9 us (92%)
  local copies, waits for them, and re-layouts  2.38 us (4%)
  between operations  1.81 us (3%)
    pallas_call x1, Pallas kernels, local(): pl.pallas_call(functools.partial(kernel, sizes), out_shape=(full, full, f...  51.9 us
    unnamed x3, local copies, waits for them, and re-layouts  2.38 us

commit v1 on v0

v1 whole, which is shorter than its diff:
```python
import functools

import jax
import jax.numpy as jnp
from jax import lax
from jax.experimental import pallas as pl
from jax.experimental.pallas import tpu as pltpu
from jax.sharding import PartitionSpec as P

WIN = 50
CAP_LEVELS = 8
ITERS = 3

step_eta = 0.4
low_density = 0.35
high_density = 0.65
layer_gap = 0.15
tiny_term = 1e-06

HALF = WIN // 2
HALO = -(-HALF // 16) * 16
TILE = 128
MESH = pl.DeviceIdType.MESH
DIRS = ((-1, 0), (1, 0), (0, -1), (0, 1), (-1, -1), (-1, 1), (1, -1), (1, 1))
ROWS_IN = (0, 1)
REST_IN = (4, 5, 6, 7, 2, 3)
EDGE = (4, 5, 6, 7, 0, 1)
SIDE = (2, 3)
F32 = jnp.float32
BF16 = jnp.bfloat16
NT = (((1,), (1,)), ((), ()))
NN = (((1,), (0,)), ((), ()))


def split(value):
    high = value.astype(BF16)
    low = (value - high.astype(F32)).astype(BF16)
    return high, low


def dot(left, right, dims=NN):
    return lax.dot_general(left, right, dims, preferred_element_type=F32)


def iota(shape, dim):
    return lax.broadcasted_iota(jnp.int32, shape, dim)


def window(offset, start):
    return jnp.where((offset >= start) & (offset < start + WIN), 1.0, 0.0).astype(BF16)


def kernel(
    sizes, cost_in, dens_in, capc_in, blocked_in, x_in, y_in, z_in,
    x, y_out, z, weight_out,
    cost, dens, capc, blocked,
    ext_u, ext_y, et_u, et_y, ht_u, ht_y, above, below, zlow, cap, grad, part,
    band_r, band_h, inner, outer, pick, slots,
    load_sem, send_sem, recv_sem, first_sem, zsend, zrecv, sum_sem, ready,
):
    nl, nr, nc = sizes
    layers, rows, cols = x_in.shape
    top = layers - 1
    ndev = nl * nr * nc
    il, ir, ic = lax.axis_index("layer"), lax.axis_index("row"), lax.axis_index("col")
    me = (il * nr + ir) * nc + ic
    tiles = rows // TILE
    order = list(dict.fromkeys((0, tiles - 1, *range(tiles))))
    ends = order[:2]
    inverse_area = 1.0 / (WIN * WIN)
    own = pl.ds(HALO, rows)
    has_above, has_below = il < nl - 1, il > 0

    pairs = (
        (y_in, ext_y.at[:, own, :]), (z_in, z), (x_in, x), (cost_in, cost), (capc_in, capc),
        (blocked_in, blocked), (dens_in, dens),
    )
    loads = [pltpu.make_async_copy(a, b, load_sem.at[n]) for n, (a, b) in enumerate(pairs)]
    for load in loads:
        load.start()

    for ref in (ext_u, ext_y):
        ref[:, :HALO, :] = jnp.zeros((layers, HALO, cols), F32)
        ref[:, HALO + rows :, :] = jnp.zeros((layers, HALO, cols), F32)
    for ref in (ht_u, ht_y, above, below, zlow):
        ref[...] = jnp.zeros(ref.shape, F32)

    barrier = pltpu.get_barrier_semaphore()

    def ahead(act):
        def one(k, _):
            i = lax.rem(me + k, ndev)
            act((i // (nr * nc), (i // nc) % nr, i % nc))
            return 0

        lax.fori_loop(1, ndev, one, 0, unroll=ndev <= 32)

    def lines(act):
        for n in range(1, nl):
            act((lax.rem(il + n, nl), ir, ic))
        for n in range(1, nr):
            act((il, lax.rem(ir + n, nr), ic))
        for n in range(1, nc):
            act((il, ir, lax.rem(ic + n, nc)))

    line_peers = nl + nr + nc - 3
    corners = []
    for dr, dc in DIRS[4:]:
        there = jnp.logical_and(
            ir < nr - 1 if dr > 0 else ir > 0, ic < nc - 1 if dc > 0 else ic > 0
        )
        corners.append((there, (il, ir + dr, ic + dc)))

    def greet(device):
        pl.semaphore_signal(barrier, inc=1, device_id=device, device_id_type=MESH)

    lines(greet)
    for there, device in corners:
        pl.when(there)(functools.partial(greet, device))

    keep_top = jnp.where(has_above, 1.0, 0.0).astype(F32)
    keep_low = jnp.where(has_below, 1.0, 0.0).astype(F32)
    shape = (2 * HALO, cols)
    k = iota(shape, 0)
    place = jnp.where(k < HALO, k, k - 2 * HALO + cols)
    pick[...] = jnp.where(place == iota(shape, 1), 1.0, 0.0).astype(BF16)

    def span(t, base=0):
        return pl.ds(t * TILE + base, TILE)

    def put_edges(et, l, t, value):
        et[l, :, span(t)] = dot(pick[...], value.astype(BF16), NT)

    loads[0].wait()
    for t in range(tiles):
        for l in range(layers):
            put_edges(et_y, l, t, ext_y[l, span(t, HALO), :])

    pl.semaphore_wait(barrier, line_peers + sum(there.astype(jnp.int32) for there, _ in corners))

    def copies(field):
        ext, et, ht = ((ext_u, et_u, ht_u), (ext_y, et_y, ht_y))[field]
        result = []
        for d, (dr, dc) in enumerate(DIRS):
            from_rows = pl.ds(0 if dc < 0 else HALO, HALO)
            to_rows = pl.ds(HALO if dc < 0 else 0, HALO)

            def ends_of(some, t, dr=dr, dc=dc, from_rows=from_rows, to_rows=to_rows):
                if dc == 0:
                    return (
                        ext.at[some, pl.ds(HALO if dr < 0 else rows, HALO), :],
                        ext.at[some, pl.ds(HALO + rows if dr < 0 else 0, HALO), :],
                    )
                if dr == 0:
                    if t is None:
                        return et.at[some, from_rows, :], ht.at[some, to_rows, pl.ds(TILE, rows)]
                    return et.at[some, from_rows, span(t)], ht.at[some, to_rows, span(t, TILE)]
                if dr < 0:
                    return (
                        et.at[some, from_rows, pl.ds(0, TILE)],
                        ht.at[some, to_rows, pl.ds(TILE + rows, TILE)],
                    )
                return (
                    et.at[some, from_rows, pl.ds(rows - TILE, TILE)],
                    ht.at[some, to_rows, pl.ds(0, TILE)],
                )

            def make(some, t=None, d=d, dr=dr, dc=dc, ends_of=ends_of):
                src, dst = ends_of(some, t)
                return pltpu.make_async_remote_copy(
                    src_ref=src, dst_ref=dst, send_sem=send_sem.at[field, d],
                    recv_sem=recv_sem.at[field, d],
                    device_id=(il, ir + dr, ic + dc), device_id_type=MESH,
                )

            to, frm = [], []
            if dr < 0:
                to.append(ir > 0)
                frm.append(ir < nr - 1)
            if dr > 0:
                to.append(ir < nr - 1)
                frm.append(ir > 0)
            if dc < 0:
                to.append(ic > 0)
                frm.append(ic < nc - 1)
            if dc > 0:
                to.append(ic < nc - 1)
                frm.append(ic > 0)
            result.append(
                (make, functools.reduce(jnp.logical_and, to), functools.reduce(jnp.logical_and, frm))
            )
        return result

    halo_copies = (copies(0), copies(1))
    every = slice(None)

    def begin(field, which, some, t=None):
        for d in which:
            make, to, _ = halo_copies[field][d]
            pl.when(to)(lambda make=make: make(some, t).start())

    def arrived(field, which):
        for d in which:
            make, _, frm = halo_copies[field][d]
            pl.when(frm)(lambda make=make: make(every).wait_recv())

    def departed(field):
        for make, to, _ in halo_copies[field]:
            pl.when(to)(lambda make=make: make(every).wait_send())

    begin(1, SIDE, every)
    begin(1, EDGE, every)

    def first_up(t):
        return pltpu.make_async_remote_copy(
            src_ref=z_in.at[top, span(t), :], dst_ref=zlow.at[span(t), :],
            send_sem=first_sem.at[0, t], recv_sem=first_sem.at[1, t],
            device_id=(il + 1, ir, ic), device_id_type=MESH,
        )

    for t in order:
        pl.when(has_above)(lambda t=t: first_up(t).start())

    def tell(n):
        def one(device):
            pl.semaphore_signal(ready.at[n], inc=1, device_id=device, device_id_type=MESH)

        lines(one)

    tell(0)

    def up(step, t):
        side = step % 2
        return pltpu.make_async_remote_copy(
            src_ref=ext_u.at[top, span(t, HALO), :], dst_ref=below.at[side, span(t), :],
            send_sem=zsend.at[side, 0, t], recv_sem=zrecv.at[side, 0, t],
            device_id=(il + 1, ir, ic), device_id_type=MESH,
        )

    def down(step, t):
        side = step % 2
        return pltpu.make_async_remote_copy(
            src_ref=ext_u.at[0, span(t, HALO), :], dst_ref=above.at[side, span(t), :],
            send_sem=zsend.at[side, 1, t], recv_sem=zrecv.at[side, 1, t],
            device_id=(il - 1, ir, ic), device_id_type=MESH,
        )

    width = layers * 2 * HALO
    for which, start in ((0, -HALF), (1, 1 - HALF)):
        shape = (TILE, TILE + 2 * HALO)
        band_r[which] = window(iota(shape, 1) - HALO - iota(shape, 0), start)
        shape = (TILE, 3 * TILE)
        band_h[which] = window(iota(shape, 1) - TILE - iota(shape, 0), start)
        shape = (cols, cols)
        own_cols = window(iota(shape, 0) - iota(shape, 1), start)
        shape = (2 * HALO, cols)
        k = iota(shape, 0)
        place = jnp.where(k < HALO, k - HALO, k - HALO + cols)
        halo_cols = window(place - iota(shape, 1), start)
        blank = jnp.zeros(shape, BF16)
        for n in range(2):
            inner[which, n * cols : (n + 1) * cols] = own_cols
            for m in range(layers):
                at = n * width + m * 2 * HALO
                for l in range(layers):
                    outer[which, at : at + 2 * HALO, l * cols : (l + 1) * cols] = (
                        halo_cols if m == l else blank
                    )

    def box_own(ext, which, t):
        tall = pl.ds(t * TILE, TILE + 2 * HALO)
        wide = jnp.concatenate([ext[l, tall, :].astype(BF16) for l in range(layers)], axis=1)
        mid = dot(band_r[which], wide)
        pieces = [
            jnp.concatenate(split(mid[:, l * cols : (l + 1) * cols]), axis=1) for l in range(layers)
        ]
        area = dot(jnp.concatenate(pieces, axis=0), inner[which])
        for l in range(layers):
            part[l, span(t), :] = area[l * TILE : (l + 1) * TILE]

    def box_early(field, which):
        ext = (ext_u, ext_y)[field]
        for t in range(tiles):
            if t not in ends:
                box_own(ext, which, t)
        arrived(field, ROWS_IN)
        for t in ends:
            box_own(ext, which, t)
        arrived(field, REST_IN)

    def box_late(ht, which, t):
        halo = ht[:, :, t * TILE : (t + 3) * TILE].reshape(width, 3 * TILE)
        side = dot(band_h[which], halo.astype(BF16), NT)
        area = dot(jnp.concatenate(split(side), axis=1), outer[which])
        return [part[l, span(t), :] + area[:, l * cols : (l + 1) * cols] for l in range(layers)]

    loads[1].wait()
    z[top] = z[top] * keep_top
    for n in range(2, 7):
        loads[n].wait()
    everywhere = [(l, t, (l, span(t), slice(None))) for t in order for l in range(layers)]
    for l, t, at in everywhere:
        level = (capc[at] + 1).astype(F32) * (1.0 / CAP_LEVELS)
        cap[at] = jnp.where(blocked[at] == 1, 0.0, level)

    def fold(value):
        return jnp.sum((value * value).reshape(TILE // 8, 8, cols), axis=0)

    def sums_begin(step, primal_sum, dual_sum):
        slots[step, pl.ds(me, 1)] = jnp.concatenate(
            [jnp.sum(primal_sum, axis=0, keepdims=True), jnp.sum(dual_sum, axis=0, keepdims=True)],
            axis=0,
        )[None]

        def send(device):
            pltpu.make_async_remote_copy(
                src_ref=slots.at[step, me], dst_ref=slots.at[step, me],
                send_sem=sum_sem.at[0, step], recv_sem=sum_sem.at[1, step],
                device_id=device, device_id_type=MESH,
            ).start()

        ahead(send)

    def sums_end(step, weight):
        some = slots.at[step, pl.ds(0, ndev - 1)]
        pltpu.make_async_copy(some, some, sum_sem.at[1, step]).wait()
        pltpu.make_async_copy(some, some, sum_sem.at[0, step]).wait()
        both = jnp.sum(slots[step], axis=0)
        primal = jnp.sum(both[0:1], axis=1, keepdims=True)
        dual = jnp.sum(both[1:2], axis=1, keepdims=True)
        ratio = jnp.broadcast_to((dual + tiny_term) / (primal + tiny_term), (1, cols))
        return jnp.sqrt(weight) * jnp.sqrt(jnp.sqrt(ratio))

    weight = jnp.ones((1, cols), F32)
    for step in range(ITERS):
        last = step == ITERS - 1
        now = step % 2
        count = (tiles * 3 // 4) if step == 0 else tiles // 2
        lower, upper = order[:count], order[count:]

        box_early(1, 1)
        for t in order:
            for l, area in enumerate(box_late(ht_y, 1, t)):
                at = (l, span(t), slice(None))
                value = cost[at] + area * inverse_area + z[at]
                grad[at] = value if l == 0 else value - z[l - 1, span(t), :]
        if step == 0:
            pl.semaphore_wait(ready.at[0], line_peers)
            tell(1)
        if step > 0:
            weight = sums_end(step - 1, weight)
        tau = step_eta / weight
        sigma = step_eta * weight
        sigma_inverse = 1.0 / sigma

        primal_sum = jnp.zeros((8, cols), F32)
        if step == 0:
            sweep = [(l, t) for l in range(1, layers) for t in order] + [(0, t) for t in order]
        else:
            sweep = [(l, t) for t in order for l in reversed(range(layers))]
        for l, t in sweep:
            at = (l, span(t), slice(None))
            slope = grad[at]
            if l == 0:
                if step == 0:
                    pl.when(has_below)(lambda t=t: first_up(t).wait_recv())
                slope = slope - zlow[span(t), :]
            old = x[at]
            new = jnp.minimum(jnp.maximum(old - tau * slope, 0.0), cap[at])
            moved = new - old
            x[at] = new
            primal_sum = primal_sum + fold(moved)
            value = new + moved + dens[at]
            ext_u[l, span(t, HALO), :] = value
            if l == top and t in upper:
                pl.when(has_above)(lambda t=t: up(step, t).start())
            if l == 0:
                pl.when(has_below)(lambda t=t: down(step, t).start())
            put_edges(et_u, l, t, value)
            begin(0, SIDE, l, t)
            if t == ends[-1]:
                begin(0, EDGE, l)
        if not last:
            for t in lower:
                pl.when(has_above)(lambda t=t: up(step, t).start())
        departed(1)
        if step == 0:
            for t in order:
                pl.when(has_above)(lambda t=t: first_up(t).wait_send())

        dual_sum = jnp.zeros((8, cols), F32)

        def update(old, here, later, keep):
            term = old * sigma_inverse + keep * (here - later)
            return sigma * (term - jnp.clip(term, -layer_gap, layer_gap)) * keep

        for l in range(top):
            for t in order:
                at = (l, span(t), slice(None))
                old = z[at]
                new = update(old, ext_u[l, span(t, HALO), :], ext_u[l + 1, span(t, HALO), :], 1.0)
                z[at] = new
                dual_sum = dual_sum + fold(new - old)

        box_early(0, 0)
        for t in order:
            for l, area in enumerate(box_late(ht_u, 0, t)):
                at = (l, span(t), slice(None))
                old = ext_y[l, span(t, HALO), :]
                term = old * sigma_inverse + area * inverse_area
                capped = jnp.minimum(term, high_density)
                clipped = jnp.where(blocked[at] == 0, jnp.maximum(capped, low_density), capped)
                new = sigma * (term - clipped)
                dual_sum = dual_sum + fold(new - old)
                if last:
                    y_out[at] = new
                else:
                    ext_y[l, span(t, HALO), :] = new
                    put_edges(et_y, l, t, new)
                    begin(1, SIDE, l, t)
                    if t == ends[-1]:
                        begin(1, EDGE, l)

        def update_top(t):
            pl.when(has_above)(lambda: down(step, t).wait_recv())
            at = (top, span(t), slice(None))
            old = z[at]
            new = update(old, ext_u[top, span(t, HALO), :], above[now, span(t), :], keep_top)
            z[at] = new
            return fold(new - old)

        def update_low(t):
            pl.when(has_below)(lambda: up(step, t).wait_recv())
            old = zlow[span(t), :]
            new = update(old, below[now, span(t), :], ext_u[0, span(t, HALO), :], keep_low)
            zlow[span(t), :] = new
            return fold(new - old)

        for t in lower:
            dual_sum = dual_sum + update_top(t)
        for t in upper:
            dual_sum = dual_sum + update_low(t)
        if step == 0:
            pl.semaphore_wait(ready.at[1], line_peers)
        sums_begin(step, primal_sum, dual_sum)
        for t in upper:
            update_top(t)
        if not last:
            for t in lower:
                update_low(t)
        for t in order:
            pl.when(has_below)(lambda t=t: down(step, t).wait_send())
            if t in upper or not last:
                pl.when(has_above)(lambda t=t: up(step, t).wait_send())
        departed(0)

    weight_out[...] = sums_end(ITERS - 1, weight)


def flush(*refs):
    count = len(refs) // 2
    ins, outs, sem = refs[:count], refs[count : 2 * count], refs[2 * count]
    moves = [
        pltpu.make_async_copy(a.at[l], b.at[l], sem.at[n, l])
        for n, (a, b) in enumerate(zip(ins, outs))
        for l in range(a.shape[0])
    ]
    for move in moves:
        move.start()
    for move in moves:
        move.wait()


def local(sizes, *args):
    layers, rows, cols = args[0].shape
    ndev = sizes[0] * sizes[1] * sizes[2]
    tiles = rows // TILE
    vmem = pl.BlockSpec(memory_space=pltpu.VMEM)
    anywhere = pl.BlockSpec(memory_space=pl.ANY)
    full = pltpu.VMEM((layers, rows, cols), F32)
    full_int = pltpu.VMEM((layers, rows, cols), jnp.int32)
    line = pltpu.VMEM((1, cols), F32)
    ext = pltpu.VMEM((layers, rows + 2 * HALO, cols), F32)
    et = pltpu.VMEM((layers, 2 * HALO, rows), F32)
    ht = pltpu.VMEM((layers, 2 * HALO, rows + 2 * TILE), F32)
    plane = pltpu.VMEM((rows, cols), F32)
    planes = pltpu.VMEM((2, rows, cols), F32)
    x, y, z, weight = pl.pallas_call(
        functools.partial(kernel, sizes),
        out_shape=(full, full, full, line),
        in_specs=[anywhere] * 7,
        out_specs=(vmem,) * 4,
        scratch_shapes=[
            full, full, full_int, full_int,
            ext, ext, et, et, ht, ht, planes, planes, plane, full, full, full,
            pltpu.VMEM((2, TILE, TILE + 2 * HALO), BF16),
            pltpu.VMEM((2, TILE, 3 * TILE), BF16),
            pltpu.VMEM((2, 2 * cols, cols), BF16),
            pltpu.VMEM((2, 2 * layers * 2 * HALO, layers * cols), BF16),
            pltpu.VMEM((2 * HALO, cols), BF16),
            pltpu.VMEM((ITERS, ndev, 2, cols), F32),
            pltpu.SemaphoreType.DMA((7,)),
            pltpu.SemaphoreType.DMA((2, 8)),
            pltpu.SemaphoreType.DMA((2, 8)),
            pltpu.SemaphoreType.DMA((2, tiles)),
            pltpu.SemaphoreType.DMA((2, 2, tiles)),
            pltpu.SemaphoreType.DMA((2, 2, tiles)),
            pltpu.SemaphoreType.DMA((2, ITERS)),
            pltpu.SemaphoreType.REGULAR((2,)),
        ],
        compiler_params=pltpu.CompilerParams(collective_id=0, has_side_effects=True),
        name="fill_steps",
    )(*args)
    whole = jax.ShapeDtypeStruct((layers, rows, cols), F32)
    x, y, z = pl.pallas_call(
        flush,
        out_shape=(whole,) * 3,
        in_specs=[anywhere] * 3,
        out_specs=(anywhere,) * 3,
        scratch_shapes=[pltpu.SemaphoreType.DMA((3, layers))],
        name="flush",
    )(*(pltpu.with_memory_space_constraint(value, pltpu.VMEM) for value in (x, y, z)))
    return x, y, z, weight[0, 0]


def solution(mesh):
    sizes = tuple(mesh.shape[axis] for axis in ("layer", "row", "col"))
    spec = P("layer", "row", "col")
    return jax.shard_map(
        functools.partial(local, sizes),
        mesh=mesh,
        in_specs=(spec,) * 7,
        out_specs=(spec, spec, spec, P()),
        check_vma=False,
    )
```

time: 56.3 us -> 49.2 us (0.87)
  Pallas kernels: 51.9 us -> 47.2 us
  local copies, waits for them, and re-layouts: 2.38 us -> 0 us
    pallas_call x1, Pallas kernels: 51.9 us -> 46 us  [local(): pl.pallas_call(functools.partial(kernel, sizes), out_shape=(full, full, f...]
    unnamed x3 -> x0, local copies, waits for them, and re-layouts: 2.38 us -> none
    pallas_call x0 -> x1, Pallas kernels: none -> 1.19 us  [local(): pl.pallas_call(flush, out_shape=(whole,) * 3, in_specs=[anywhere] * 3, ou...]
where the time goes in v1:
time: 49.2 us; the launch traced here: 49 us
  Pallas kernels  47.2 us (96%)
  between operations  1.81 us (4%)
    pallas_call x1, Pallas kernels, local(): pl.pallas_call(functools.partial(kernel, sizes), out_shape=(full, full, f...  46 us
    pallas_call x1, Pallas kernels, local(): pl.pallas_call(flush, out_shape=(whole,) * 3, in_specs=[anywhere] * 3, ou...  1.19 us

profile of v1, /device:TPU:0, one launch (start us, length us, event | category | flops | bytes accessed | tf_op | source)
XLA Modules:
  0.0 49.0 jit_solution(4600044663165283542)
XLA Ops:
  0.6 46.0 %fill_steps.1 = (f32[2,512,128]{2,1,0:T(8,128)S(1)}, f32[2,512,128]{2,1,0:T(8,128)S(1)}, f32[2,512,128]{2,1,0:T(8,128)S(1)}, f32[1,128]{1,0:T(1,128)S(1)}) custom-call(f32[2,512,128]{2,1,0:T(8,128)} %cost_in.1, f32[2,512,128]{2,1,0:T(8,128)} %dens_in.1, s32[2,512,128]{2,1,0:T(8,128)} %capc_in.1, s32[2,512,128]{2,1,0:T(8,128)} %blocked_in.1, ...), custom_call_target="tpu_custom_call" | custom-call | tf_op jit(solution)/shard_map/fill_steps/pallas_call | solution.py:488
  46.7 1.2 %flush.1 = (f32[2,512,128]{2,1,0:T(8,128)}, f32[2,512,128]{2,1,0:T(8,128)}, f32[2,512,128]{2,1,0:T(8,128)}) custom-call(f32[2,512,128]{2,1,0:T(8,128)S(1)} %get-tuple-element.11.refs_0_, f32[2,512,128]{2,1,0:T(8,128)S(1)} %get-tuple-element.12.refs_1_, f32[2,512,128]{2,1,0:T(8,128)S(1)} %get-tuple-element.13.refs_2_), custom_call_target="tpu_custom_call" | custom-call | tf_op jit(solution)/shard_map/flush/pallas_call | solution.py:515

commit v2 on v1

--- a/solution.py
+++ b/solution.py
@@ -21,11 +21,11 @@
 HALO = -(-HALF // 16) * 16
 TILE = 128
 MESH = pl.DeviceIdType.MESH
+HBM = "hbm"
 DIRS = ((-1, 0), (1, 0), (0, -1), (0, 1), (-1, -1), (-1, 1), (1, -1), (1, 1))
-ROWS_IN = (0, 1)
-REST_IN = (4, 5, 6, 7, 2, 3)
-EDGE = (4, 5, 6, 7, 0, 1)
+ROWS = (0, 1)
 SIDE = (2, 3)
+CORNER = (4, 5, 6, 7)
 F32 = jnp.float32
 BF16 = jnp.bfloat16
 NT = (((1,), (1,)), ((), ()))
@@ -50,11 +50,19 @@
     return jnp.where((offset >= start) & (offset < start + WIN), 1.0, 0.0).astype(BF16)
 
 
+def spreads(sizes):
+    distance, result = 1, []
+    while distance < max(sizes) - 1:
+        result.append(distance)
+        distance *= 2
+    return result
+
+
 def kernel(
     sizes, cost_in, dens_in, capc_in, blocked_in, x_in, y_in, z_in,
     x, y_out, z, weight_out,
-    cost, dens, capc, blocked,
-    ext_u, ext_y, et_u, et_y, ht_u, ht_y, above, below, zlow, cap, grad, part,
+    reals, flags,
+    ext_u, ext_y, et_u, et_y, ht_u, ht_y, ct_u, ct_y, above, below, zlow, cap, grad, part,
     band_r, band_h, inner, outer, pick, slots,
     load_sem, send_sem, recv_sem, first_sem, zsend, zrecv, sum_sem, ready,
 ):
@@ -64,25 +72,30 @@
     ndev = nl * nr * nc
     il, ir, ic = lax.axis_index("layer"), lax.axis_index("row"), lax.axis_index("col")
     me = (il * nr + ir) * nc + ic
+    cost, dens, capc, blocked = reals.at[0], reals.at[1], flags.at[0], flags.at[1]
     tiles = rows // TILE
     order = list(dict.fromkeys((0, tiles - 1, *range(tiles))))
     ends = order[:2]
+    rest = order[2:]
     inverse_area = 1.0 / (WIN * WIN)
     own = pl.ds(HALO, rows)
     has_above, has_below = il < nl - 1, il > 0
 
     pairs = (
-        (y_in, ext_y.at[:, own, :]), (z_in, z), (x_in, x), (cost_in, cost), (capc_in, capc),
-        (blocked_in, blocked), (dens_in, dens),
+        (y_in, ext_y.at[:, own, :], 0), (z_in, z, 1), (cost_in, cost, 2), (dens_in, dens, 2),
+        (x_in, x, 3), (capc_in, capc, 4), (blocked_in, blocked, 4),
     )
-    loads = [pltpu.make_async_copy(a, b, load_sem.at[n]) for n, (a, b) in enumerate(pairs)]
-    for load in loads:
-        load.start()
+    for a, b, n in pairs:
+        pltpu.make_async_copy(a, b, load_sem.at[n]).start()
+    loads = [
+        pltpu.make_async_copy(ref, ref, load_sem.at[n])
+        for n, ref in enumerate((ext_y.at[:, own, :], z, reals, x, flags))
+    ]
 
     for ref in (ext_u, ext_y):
         ref[:, :HALO, :] = jnp.zeros((layers, HALO, cols), F32)
         ref[:, HALO + rows :, :] = jnp.zeros((layers, HALO, cols), F32)
-    for ref in (ht_u, ht_y, above, below, zlow):
+    for ref in (ht_u, ht_y, ct_u, ct_y, above, below, zlow):
         ref[...] = jnp.zeros(ref.shape, F32)
 
     barrier = pltpu.get_barrier_semaphore()
@@ -103,6 +116,16 @@
         for n in range(1, nc):
             act((il, ir, lax.rem(ic + n, nc)))
 
+    def beside(distance):
+        peers = []
+        for axis, (at, n) in enumerate(((il, nl), (ir, nr), (ic, nc))):
+            if distance < n:
+                for there, to in ((at >= distance, at - distance), (at < n - distance, at + distance)):
+                    device = [il, ir, ic]
+                    device[axis] = to
+                    peers.append((there, tuple(device)))
+        return peers
+
     line_peers = nl + nr + nc - 3
     corners = []
     for dr, dc in DIRS[4:]:
@@ -111,12 +134,53 @@
         )
         corners.append((there, (il, ir + dr, ic + dc)))
 
-    def greet(device):
-        pl.semaphore_signal(barrier, inc=1, device_id=device, device_id_type=MESH)
-
-    lines(greet)
-    for there, device in corners:
-        pl.when(there)(functools.partial(greet, device))
+    def signal(semaphore, device):
+        pl.semaphore_signal(semaphore, inc=1, device_id=device, device_id_type=MESH)
+
+    def signal_some(semaphore, peers):
+        for there, device in peers:
+            pl.when(there)(functools.partial(signal, semaphore, device))
+
+    def wait_some(semaphore, peers):
+        pl.semaphore_wait(semaphore, sum(there.astype(jnp.int32) for there, _ in peers))
+
+    signal_some(barrier, beside(1) + corners)
+
+    spread = spreads(sizes)
+    rounds = len(spread) + 2
+
+    def tell(n):
+        if n < len(spread):
+            signal_some(ready.at[n], beside(spread[n]))
+        elif n < rounds:
+            lines(functools.partial(signal, ready.at[n]))
+
+    def hear(n):
+        if n < len(spread):
+            wait_some(ready.at[n], beside(spread[n]))
+        elif n < rounds:
+            pl.semaphore_wait(ready.at[n], line_peers)
+        tell(n + 1)
+
+    def span(t, base=0):
+        return pl.ds(t * TILE + base, TILE)
+
+    wait_some(barrier, beside(1) + corners)
+
+    def first_up(t):
+        return pltpu.make_async_remote_copy(
+            src_ref=z_in.at[top, span(t), :], dst_ref=zlow.at[span(t), :],
+            send_sem=first_sem.at[tiles], recv_sem=first_sem.at[t],
+            device_id=(il + 1, ir, ic), device_id_type=MESH,
+        )
+
+    @pl.when(has_above)
+    def _():
+        for t in order:
+            first_up(t).start()
+
+
+    tell(0)
 
     keep_top = jnp.where(has_above, 1.0, 0.0).astype(F32)
     keep_low = jnp.where(has_below, 1.0, 0.0).astype(F32)
@@ -125,21 +189,26 @@
     place = jnp.where(k < HALO, k, k - 2 * HALO + cols)
     pick[...] = jnp.where(place == iota(shape, 1), 1.0, 0.0).astype(BF16)
 
-    def span(t, base=0):
-        return pl.ds(t * TILE + base, TILE)
-
     def put_edges(et, l, t, value):
-        et[l, :, span(t)] = dot(pick[...], value.astype(BF16), NT)
-
-    loads[0].wait()
-    for t in range(tiles):
+        turned = value.T
+        et[l, :HALO, span(t)] = turned[:HALO]
+        et[l, HALO:, span(t)] = turned[cols - HALO :]
+
+    def put_corners(ct, first, final):
+        blank = jnp.zeros((TILE - layers * HALO, cols), F32)
+        for n, pieces in enumerate(
+            ([value[:HALO] for value in first], [value[TILE - HALO :] for value in final])
+        ):
+            ct[0, n] = dot(pick[...], jnp.concatenate(pieces + [blank], axis=0).astype(BF16), NT)
+
+    def take_corners(ct, ht):
         for l in range(layers):
-            put_edges(et_y, l, t, ext_y[l, span(t, HALO), :])
-
-    pl.semaphore_wait(barrier, line_peers + sum(there.astype(jnp.int32) for there, _ in corners))
+            ht[l, :, :TILE] = pltpu.roll(ct[1, 1], TILE - (l + 1) * HALO, axis=1)
+            last_tile = ct[1, 0]
+            ht[l, :, TILE + rows :] = pltpu.roll(last_tile, TILE - l * HALO, axis=1) if l else last_tile
 
     def copies(field):
-        ext, et, ht = ((ext_u, et_u, ht_u), (ext_y, et_y, ht_y))[field]
+        ext, et, ht, ct = ((ext_u, et_u, ht_u, ct_u), (ext_y, et_y, ht_y, ct_y))[field]
         result = []
         for d, (dr, dc) in enumerate(DIRS):
             from_rows = pl.ds(0 if dc < 0 else HALO, HALO)
@@ -148,22 +217,16 @@
             def ends_of(some, t, dr=dr, dc=dc, from_rows=from_rows, to_rows=to_rows):
                 if dc == 0:
                     return (
-                        ext.at[some, pl.ds(HALO if dr < 0 else rows, HALO), :],
+                        y_in.at[some, pl.ds(0 if dr < 0 else rows - HALO, HALO), :] if t is HBM
+                        else ext.at[some, pl.ds(HALO if dr < 0 else rows, HALO), :],
                         ext.at[some, pl.ds(HALO + rows if dr < 0 else 0, HALO), :],
                     )
                 if dr == 0:
                     if t is None:
                         return et.at[some, from_rows, :], ht.at[some, to_rows, pl.ds(TILE, rows)]
                     return et.at[some, from_rows, span(t)], ht.at[some, to_rows, span(t, TILE)]
-                if dr < 0:
-                    return (
-                        et.at[some, from_rows, pl.ds(0, TILE)],
-                        ht.at[some, to_rows, pl.ds(TILE + rows, TILE)],
-                    )
-                return (
-                    et.at[some, from_rows, pl.ds(rows - TILE, TILE)],
-                    ht.at[some, to_rows, pl.ds(0, TILE)],
-                )
+                n = 0 if dr < 0 else 1
+                return ct.at[0, n, from_rows, :], ct.at[1, n, to_rows, :]
 
             def make(some, t=None, d=d, dr=dr, dc=dc, ends_of=ends_of):
                 src, dst = ends_of(some, t)
@@ -194,10 +257,14 @@
     halo_copies = (copies(0), copies(1))
     every = slice(None)
 
-    def begin(field, which, some, t=None):
+    def begin(field, which, some, some_tiles=(None,)):
         for d in which:
             make, to, _ = halo_copies[field][d]
-            pl.when(to)(lambda make=make: make(some, t).start())
+
+            @pl.when(to)
+            def _(make=make):
+                for t in some_tiles:
+                    make(some, t).start()
 
     def arrived(field, which):
         for d in which:
@@ -208,32 +275,26 @@
         for make, to, _ in halo_copies[field]:
             pl.when(to)(lambda make=make: make(every).wait_send())
 
-    begin(1, SIDE, every)
-    begin(1, EDGE, every)
-
-    def first_up(t):
-        return pltpu.make_async_remote_copy(
-            src_ref=z_in.at[top, span(t), :], dst_ref=zlow.at[span(t), :],
-            send_sem=first_sem.at[0, t], recv_sem=first_sem.at[1, t],
-            device_id=(il + 1, ir, ic), device_id_type=MESH,
-        )
-
-    for t in order:
-        pl.when(has_above)(lambda t=t: first_up(t).start())
-
-    def tell(n):
-        def one(device):
-            pl.semaphore_signal(ready.at[n], inc=1, device_id=device, device_id_type=MESH)
-
-        lines(one)
-
-    tell(0)
+    begin(1, ROWS, every, (HBM,))
+    loads[0].wait()
+    for t in range(tiles):
+        for l in range(layers):
+            put_edges(et_y, l, t, ext_y[l, span(t, HALO), :])
+    put_corners(
+        ct_y,
+        [ext_y[l, span(0, HALO), :] for l in range(layers)],
+        [ext_y[l, span(tiles - 1, HALO), :] for l in range(layers)],
+    )
+    begin(1, SIDE + CORNER, every)
+
+    def lower_of(step):
+        return order[: tiles // 2]
 
     def up(step, t):
         side = step % 2
         return pltpu.make_async_remote_copy(
             src_ref=ext_u.at[top, span(t, HALO), :], dst_ref=below.at[side, span(t), :],
-            send_sem=zsend.at[side, 0, t], recv_sem=zrecv.at[side, 0, t],
+            send_sem=zsend.at[side, 0], recv_sem=zrecv.at[side, 0, int(t in lower_of(step))],
             device_id=(il + 1, ir, ic), device_id_type=MESH,
         )
 
@@ -241,7 +302,7 @@
         side = step % 2
         return pltpu.make_async_remote_copy(
             src_ref=ext_u.at[0, span(t, HALO), :], dst_ref=above.at[side, span(t), :],
-            send_sem=zsend.at[side, 1, t], recv_sem=zrecv.at[side, 1, t],
+            send_sem=zsend.at[side, 1], recv_sem=zrecv.at[side, 1, int(t not in lower_of(step))],
             device_id=(il - 1, ir, ic), device_id_type=MESH,
         )
 
@@ -278,15 +339,18 @@
         for l in range(layers):
             part[l, span(t), :] = area[l * TILE : (l + 1) * TILE]
 
-    def box_early(field, which):
+    def box_early(field, which, then=None):
         ext = (ext_u, ext_y)[field]
         for t in range(tiles):
             if t not in ends:
                 box_own(ext, which, t)
-        arrived(field, ROWS_IN)
+        arrived(field, ROWS)
+        if then is not None:
+            then()
         for t in ends:
             box_own(ext, which, t)
-        arrived(field, REST_IN)
+        arrived(field, CORNER + SIDE)
+        take_corners((ct_u, ct_y)[field], (ht_u, ht_y)[field])
 
     def box_late(ht, which, t):
         halo = ht[:, :, t * TILE : (t + 3) * TILE].reshape(width, 3 * TILE)
@@ -296,8 +360,8 @@
 
     loads[1].wait()
     z[top] = z[top] * keep_top
-    for n in range(2, 7):
-        loads[n].wait()
+    for load in loads[2:]:
+        load.wait()
     everywhere = [(l, t, (l, span(t), slice(None))) for t in order for l in range(layers)]
     for l, t, at in everywhere:
         level = (capc[at] + 1).astype(F32) * (1.0 / CAP_LEVELS)
@@ -335,62 +399,87 @@
     for step in range(ITERS):
         last = step == ITERS - 1
         now = step % 2
-        count = (tiles * 3 // 4) if step == 0 else tiles // 2
-        lower, upper = order[:count], order[count:]
+        lower = lower_of(step)
+        upper = [t for t in order if t not in lower]
 
         box_early(1, 1)
         for t in order:
             for l, area in enumerate(box_late(ht_y, 1, t)):
                 at = (l, span(t), slice(None))
-                value = cost[at] + area * inverse_area + z[at]
-                grad[at] = value if l == 0 else value - z[l - 1, span(t), :]
-        if step == 0:
-            pl.semaphore_wait(ready.at[0], line_peers)
-            tell(1)
+                grad[at] = cost[at] + area * inverse_area
         if step > 0:
+            finish()
             weight = sums_end(step - 1, weight)
         tau = step_eta / weight
         sigma = step_eta * weight
         sigma_inverse = 1.0 / sigma
 
         primal_sum = jnp.zeros((8, cols), F32)
+        groups = [g for g in (ends, rest) if g]
         if step == 0:
-            sweep = [(l, t) for l in range(1, layers) for t in order] + [(0, t) for t in order]
+            blocks = [(range(1, layers), g) for g in groups] + [(range(1), [t]) for t in order]
         else:
-            sweep = [(l, t) for t in order for l in reversed(range(layers))]
-        for l, t in sweep:
-            at = (l, span(t), slice(None))
-            slope = grad[at]
-            if l == 0:
-                if step == 0:
+            blocks = [(range(layers), g) for g in groups]
+        if step == 0:
+            hear(0)
+        for some_layers, some_tiles in blocks:
+            if step == 0 and 0 in some_layers:
+                for t in some_tiles:
                     pl.when(has_below)(lambda t=t: first_up(t).wait_recv())
-                slope = slope - zlow[span(t), :]
-            old = x[at]
-            new = jnp.minimum(jnp.maximum(old - tau * slope, 0.0), cap[at])
-            moved = new - old
-            x[at] = new
-            primal_sum = primal_sum + fold(moved)
-            value = new + moved + dens[at]
-            ext_u[l, span(t, HALO), :] = value
-            if l == top and t in upper:
-                pl.when(has_above)(lambda t=t: up(step, t).start())
-            if l == 0:
-                pl.when(has_below)(lambda t=t: down(step, t).start())
-            put_edges(et_u, l, t, value)
-            begin(0, SIDE, l, t)
-            if t == ends[-1]:
-                begin(0, EDGE, l)
-        if not last:
-            for t in lower:
-                pl.when(has_above)(lambda t=t: up(step, t).start())
+            for t in some_tiles:
+                for l in some_layers:
+                    at = (l, span(t), slice(None))
+                    earlier = zlow[span(t), :] if l == 0 else z[l - 1, span(t), :]
+                    slope = grad[at] + (z[at] - earlier)
+                    old = x[at]
+                    new = jnp.minimum(jnp.maximum(old - tau * slope, 0.0), cap[at])
+                    moved = new - old
+                    x[at] = new
+                    primal_sum = primal_sum + fold(moved)
+                    value = new + moved + dens[at]
+                    ext_u[l, span(t, HALO), :] = value
+                    put_edges(et_u, l, t, value)
+            first_layer = some_layers[0]
+            some = pl.ds(first_layer, len(some_layers))
+            corner_ready = 0 in some_layers and ends[-1] in some_tiles
+            if corner_ready:
+                put_corners(
+                    ct_u,
+                    [ext_u[l, span(0, HALO), :] for l in range(layers)],
+                    [ext_u[l, span(tiles - 1, HALO), :] for l in range(layers)],
+                )
+            begin(0, SIDE, some, some_tiles)
+            if ends[-1] in some_tiles:
+                begin(0, ROWS, some)
+            if corner_ready:
+                begin(0, CORNER, every)
+            if 0 in some_layers:
+
+                @pl.when(has_below)
+                def _(step=step, some_tiles=some_tiles):
+                    for t in some_tiles:
+                        if t in lower:
+                            down(step, t).start()
+
+            if top in some_layers:
+                going = [t for t in some_tiles if t in upper]
+
+                @pl.when(has_above)
+                def _(step=step, going=going):
+                    for t in going:
+                        up(step, t).start()
+
+            if step == 0:
+                if (some_layers, some_tiles) == blocks[1]:
+                    hear(1)
         departed(1)
         if step == 0:
-            for t in order:
-                pl.when(has_above)(lambda t=t: first_up(t).wait_send())
+
+            pl.when(has_above)(pltpu.make_async_copy(zlow, zlow, first_sem.at[tiles]).wait)
 
         dual_sum = jnp.zeros((8, cols), F32)
 
-        def update(old, here, later, keep):
+        def update(old, here, later, keep, sigma=sigma, sigma_inverse=sigma_inverse):
             term = old * sigma_inverse + keep * (here - later)
             return sigma * (term - jnp.clip(term, -layer_gap, layer_gap)) * keep
 
@@ -402,8 +491,31 @@
                 z[at] = new
                 dual_sum = dual_sum + fold(new - old)
 
-        box_early(0, 0)
+        def other_half(last=last, step=step, lower=lower, upper=upper):
+            @pl.when(has_below)
+            def _():
+                for t in upper:
+                    down(step, t).start()
+
+            if not last:
+
+                @pl.when(has_above)
+                def _():
+                    for t in lower:
+                        up(step, t).start()
+
+        box_early(0, 0, other_half)
+        if step == 0:
+            hear(2)
         for t in order:
+            if not last and rest and t == rest[0]:
+                put_corners(
+                    ct_y,
+                    [ext_y[l, span(0, HALO), :] for l in range(layers)],
+                    [ext_y[l, span(tiles - 1, HALO), :] for l in range(layers)],
+                )
+                begin(1, SIDE, every, ends)
+                begin(1, ROWS + CORNER, every)
             for l, area in enumerate(box_late(ht_u, 0, t)):
                 at = (l, span(t), slice(None))
                 old = ext_y[l, span(t, HALO), :]
@@ -417,43 +529,60 @@
                 else:
                     ext_y[l, span(t, HALO), :] = new
                     put_edges(et_y, l, t, new)
-                    begin(1, SIDE, l, t)
-                    if t == ends[-1]:
-                        begin(1, EDGE, l)
-
-        def update_top(t):
-            pl.when(has_above)(lambda: down(step, t).wait_recv())
+
+        if not last:
+            begin(1, SIDE, every, rest)
+
+        def update_top(t, now=now, update=update):
             at = (top, span(t), slice(None))
             old = z[at]
             new = update(old, ext_u[top, span(t, HALO), :], above[now, span(t), :], keep_top)
             z[at] = new
             return fold(new - old)
 
-        def update_low(t):
-            pl.when(has_below)(lambda: up(step, t).wait_recv())
+        def update_low(t, now=now, update=update):
             old = zlow[span(t), :]
             new = update(old, below[now, span(t), :], ext_u[0, span(t, HALO), :], keep_low)
             zlow[span(t), :] = new
             return fold(new - old)
 
+        def landed(downs, ups, now=now, lower=lower):
+            for there, plane, way, some in (
+                (has_above, above, 1, downs), (has_below, below, 0, ups)
+            ):
+                if some:
+                    all_of = plane.at[now, pl.ds(0, len(some) * TILE), :]
+                    which = int((some == lower) == (way == 0))
+                    pl.when(there)(
+                        pltpu.make_async_copy(all_of, all_of, zrecv.at[now, way, which]).wait
+                    )
+
+        landed(lower, upper)
         for t in lower:
             dual_sum = dual_sum + update_top(t)
         for t in upper:
             dual_sum = dual_sum + update_low(t)
         if step == 0:
-            pl.semaphore_wait(ready.at[1], line_peers)
+            for n in range(3, rounds):
+                hear(n)
         sums_begin(step, primal_sum, dual_sum)
-        for t in upper:
-            update_top(t)
-        if not last:
-            for t in lower:
-                update_low(t)
-        for t in order:
-            pl.when(has_below)(lambda t=t: down(step, t).wait_send())
-            if t in upper or not last:
-                pl.when(has_above)(lambda t=t: up(step, t).wait_send())
-        departed(0)
-
+
+        def finish(last=last, step=step, now=now, lower=lower, upper=upper, landed=landed,
+                   update_top=update_top, update_low=update_low):
+            landed(upper, [] if last else lower)
+            for t in upper:
+                update_top(t)
+            if not last:
+                for t in lower:
+                    update_low(t)
+
+            for there, way, gone in ((has_below, 1, order), (has_above, 0, upper if last else order)):
+                all_of = above.at[now, pl.ds(0, len(gone) * TILE), :]
+                pl.when(there)(pltpu.make_async_copy(all_of, all_of, zsend.at[now, way]).wait)
+
+            departed(0)
+
+    finish()
     weight_out[...] = sums_end(ITERS - 1, weight)
 
 
@@ -478,11 +607,13 @@
     vmem = pl.BlockSpec(memory_space=pltpu.VMEM)
     anywhere = pl.BlockSpec(memory_space=pl.ANY)
     full = pltpu.VMEM((layers, rows, cols), F32)
-    full_int = pltpu.VMEM((layers, rows, cols), jnp.int32)
+    fields = pltpu.VMEM((2, layers, rows, cols), F32)
+    field_flags = pltpu.VMEM((2, layers, rows, cols), jnp.int32)
     line = pltpu.VMEM((1, cols), F32)
     ext = pltpu.VMEM((layers, rows + 2 * HALO, cols), F32)
     et = pltpu.VMEM((layers, 2 * HALO, rows), F32)
     ht = pltpu.VMEM((layers, 2 * HALO, rows + 2 * TILE), F32)
+    ct = pltpu.VMEM((2, 2, 2 * HALO, TILE), F32)
     plane = pltpu.VMEM((rows, cols), F32)
     planes = pltpu.VMEM((2, rows, cols), F32)
     x, y, z, weight = pl.pallas_call(
@@ -491,22 +622,22 @@
         in_specs=[anywhere] * 7,
         out_specs=(vmem,) * 4,
         scratch_shapes=[
-            full, full, full_int, full_int,
-            ext, ext, et, et, ht, ht, planes, planes, plane, full, full, full,
+            fields, field_flags,
+            ext, ext, et, et, ht, ht, ct, ct, planes, planes, plane, full, full, full,
             pltpu.VMEM((2, TILE, TILE + 2 * HALO), BF16),
             pltpu.VMEM((2, TILE, 3 * TILE), BF16),
             pltpu.VMEM((2, 2 * cols, cols), BF16),
             pltpu.VMEM((2, 2 * layers * 2 * HALO, layers * cols), BF16),
             pltpu.VMEM((2 * HALO, cols), BF16),
             pltpu.VMEM((ITERS, ndev, 2, cols), F32),
-            pltpu.SemaphoreType.DMA((7,)),
+            pltpu.SemaphoreType.DMA((5,)),
             pltpu.SemaphoreType.DMA((2, 8)),
             pltpu.SemaphoreType.DMA((2, 8)),
-            pltpu.SemaphoreType.DMA((2, tiles)),
-            pltpu.SemaphoreType.DMA((2, 2, tiles)),
-            pltpu.SemaphoreType.DMA((2, 2, tiles)),
+            pltpu.SemaphoreType.DMA((tiles + 1,)),
+            pltpu.SemaphoreType.DMA((2, 2)),
+            pltpu.SemaphoreType.DMA((2, 2, 2)),
             pltpu.SemaphoreType.DMA((2, ITERS)),
-            pltpu.SemaphoreType.REGULAR((2,)),
+            pltpu.SemaphoreType.REGULAR((len(spreads(sizes)) + 2,)),
         ],
         compiler_params=pltpu.CompilerParams(collective_id=0, has_side_effects=True),
         name="fill_steps",

time: 49.2 us -> 46 us (0.935)
  Pallas kernels: 47.2 us -> 44.1 us
    pallas_call x1, Pallas kernels: 46 us -> 42.9 us  [local(): pl.pallas_call(functools.partial(kernel, sizes), out_shape=(full, full, f...]
where the time goes in v2:
time: 46 us; the launch traced here: 45.9 us
  Pallas kernels  44.1 us (96%)
  between operations  1.81 us (4%)
    pallas_call x1, Pallas kernels, local(): pl.pallas_call(functools.partial(kernel, sizes), out_shape=(full, full, f...  42.9 us
    pallas_call x1, Pallas kernels, local(): pl.pallas_call(flush, out_shape=(whole,) * 3, in_specs=[anywhere] * 3, ou...  1.19 us

profile of v2, /device:TPU:0, one launch (start us, length us, event | category | flops | bytes accessed | tf_op | source)
XLA Modules:
  0.0 45.9 jit_solution(2589762817317360608)
XLA Ops:
  0.6 42.9 %fill_steps.1 = (f32[2,512,128]{2,1,0:T(8,128)S(1)}, f32[2,512,128]{2,1,0:T(8,128)S(1)}, f32[2,512,128]{2,1,0:T(8,128)S(1)}, f32[1,128]{1,0:T(1,128)S(1)}) custom-call(f32[2,512,128]{2,1,0:T(8,128)} %cost_in.1, f32[2,512,128]{2,1,0:T(8,128)} %dens_in.1, s32[2,512,128]{2,1,0:T(8,128)} %capc_in.1, s32[2,512,128]{2,1,0:T(8,128)} %blocked_in.1, ...), custom_call_target="tpu_custom_call" | custom-call | tf_op jit(solution)/shard_map/fill_steps/pallas_call | solution.py:619
  43.5 1.2 %flush.1 = (f32[2,512,128]{2,1,0:T(8,128)}, f32[2,512,128]{2,1,0:T(8,128)}, f32[2,512,128]{2,1,0:T(8,128)}) custom-call(f32[2,512,128]{2,1,0:T(8,128)S(1)} %get-tuple-element.11.refs_0_, f32[2,512,128]{2,1,0:T(8,128)S(1)} %get-tuple-element.12.refs_1_, f32[2,512,128]{2,1,0:T(8,128)S(1)} %get-tuple-element.13.refs_2_), custom_call_target="tpu_custom_call" | custom-call | tf_op jit(solution)/shard_map/flush/pallas_call | solution.py:646

commit v3 on v2

--- a/solution.py
+++ b/solution.py
@@ -19,9 +19,11 @@
 
 HALF = WIN // 2
 HALO = -(-HALF // 16) * 16
+MOST = (HALF - 1) // 8 * 8
+assert WIN == 2 * HALF and MOST == HALF - 1
 TILE = 128
 MESH = pl.DeviceIdType.MESH
-HBM = "hbm"
+HBM, EXTRA = "hbm", "extra"
 DIRS = ((-1, 0), (1, 0), (0, -1), (0, 1), (-1, -1), (-1, 1), (1, -1), (1, 1))
 ROWS = (0, 1)
 SIDE = (2, 3)
@@ -62,7 +64,7 @@
     sizes, cost_in, dens_in, capc_in, blocked_in, x_in, y_in, z_in,
     x, y_out, z, weight_out,
     reals, flags,
-    ext_u, ext_y, et_u, et_y, ht_u, ht_y, ct_u, ct_y, above, below, zlow, cap, grad, part,
+    ext_u, ext_y, et_u, et_y, ht_u, ht_y, ct_u, ct_y, ex_u, ex_y, above, below, zlow, cap, grad, part,
     band_r, band_h, inner, outer, pick, slots,
     load_sem, send_sem, recv_sem, first_sem, zsend, zrecv, sum_sem, ready,
 ):
@@ -95,7 +97,7 @@
     for ref in (ext_u, ext_y):
         ref[:, :HALO, :] = jnp.zeros((layers, HALO, cols), F32)
         ref[:, HALO + rows :, :] = jnp.zeros((layers, HALO, cols), F32)
-    for ref in (ht_u, ht_y, ct_u, ct_y, above, below, zlow):
+    for ref in (ht_u, ht_y, ct_u, ct_y, ex_u, ex_y, above, below, zlow):
         ref[...] = jnp.zeros(ref.shape, F32)
 
     barrier = pltpu.get_barrier_semaphore()
@@ -189,8 +191,11 @@
     place = jnp.where(k < HALO, k, k - 2 * HALO + cols)
     pick[...] = jnp.where(place == iota(shape, 1), 1.0, 0.0).astype(BF16)
 
-    def put_edges(et, l, t, value):
+    def put_edges(field, l, t, value):
+        et, ex = ((et_u, ex_u), (et_y, ex_y))[field]
         turned = value.T
+        beyond = cols - HALF if field == 0 else HALF - 1
+        ex[0, l : l + 1, span(t)] = turned[beyond : beyond + 1]
         et[l, :HALO, span(t)] = turned[:HALO]
         et[l, HALO:, span(t)] = turned[cols - HALO :]
 
@@ -208,20 +213,27 @@
             ht[l, :, TILE + rows :] = pltpu.roll(last_tile, TILE - l * HALO, axis=1) if l else last_tile
 
     def copies(field):
-        ext, et, ht, ct = ((ext_u, et_u, ht_u, ct_u), (ext_y, et_y, ht_y, ct_y))[field]
+        ext, et, ht, ct, ex = (
+            (ext_u, et_u, ht_u, ct_u, ex_u), (ext_y, et_y, ht_y, ct_y, ex_y)
+        )[field]
+        longer = 1 if field == 0 else -1
         result = []
         for d, (dr, dc) in enumerate(DIRS):
-            from_rows = pl.ds(0 if dc < 0 else HALO, HALO)
-            to_rows = pl.ds(HALO if dc < 0 else 0, HALO)
-
-            def ends_of(some, t, dr=dr, dc=dc, from_rows=from_rows, to_rows=to_rows):
+            wide = HALO if dr and dc == longer else MOST
+            from_rows = pl.ds(0 if dc < 0 else 2 * HALO - wide, wide)
+            to_rows = pl.ds(HALO if dc < 0 else HALO - wide, wide)
+            tall = HALO if dr == longer else MOST
+
+            def ends_of(some, t, dr=dr, dc=dc, from_rows=from_rows, to_rows=to_rows, tall=tall):
                 if dc == 0:
                     return (
-                        y_in.at[some, pl.ds(0 if dr < 0 else rows - HALO, HALO), :] if t is HBM
-                        else ext.at[some, pl.ds(HALO if dr < 0 else rows, HALO), :],
-                        ext.at[some, pl.ds(HALO + rows if dr < 0 else 0, HALO), :],
+                        y_in.at[some, pl.ds(0 if dr < 0 else rows - tall, tall), :] if t is HBM
+                        else ext.at[some, pl.ds(HALO if dr < 0 else HALO + rows - tall, tall), :],
+                        ext.at[some, pl.ds(HALO + rows if dr < 0 else HALO - tall, tall), :],
                     )
                 if dr == 0:
+                    if t is EXTRA:
+                        return ex.at[0], ex.at[1]
                     if t is None:
                         return et.at[some, from_rows, :], ht.at[some, to_rows, pl.ds(TILE, rows)]
                     return et.at[some, from_rows, span(t)], ht.at[some, to_rows, span(t, TILE)]
@@ -249,46 +261,60 @@
             if dc > 0:
                 to.append(ic < nc - 1)
                 frm.append(ic > 0)
+
+            def both(semaphore, d=d):
+                size = above.at[0, pl.ds(0, layers * HALF * rows // cols), :]
+                return pltpu.make_async_copy(size, size, semaphore.at[field, d])
+
+            if dr or dc != longer:
+                both = None
+
             result.append(
-                (make, functools.reduce(jnp.logical_and, to), functools.reduce(jnp.logical_and, frm))
+                (make, both, functools.reduce(jnp.logical_and, to), functools.reduce(jnp.logical_and, frm))
             )
         return result
 
     halo_copies = (copies(0), copies(1))
     every = slice(None)
 
-    def begin(field, which, some, some_tiles=(None,)):
+    def begin(field, which, some, some_tiles=(None,), whole=False):
         for d in which:
-            make, to, _ = halo_copies[field][d]
+            make, both, to, _ = halo_copies[field][d]
 
             @pl.when(to)
-            def _(make=make):
+            def _(make=make, both=both):
                 for t in some_tiles:
                     make(some, t).start()
+                if whole and both:
+                    make(every, EXTRA).start()
 
     def arrived(field, which):
         for d in which:
-            make, _, frm = halo_copies[field][d]
-            pl.when(frm)(lambda make=make: make(every).wait_recv())
+            make, both, _, frm = halo_copies[field][d]
+            pl.when(frm)(
+                lambda make=make, both=both: (both(recv_sem).wait() if both else make(every).wait_recv())
+            )
 
     def departed(field):
-        for make, to, _ in halo_copies[field]:
-            pl.when(to)(lambda make=make: make(every).wait_send())
+        for make, both, to, _ in halo_copies[field]:
+            pl.when(to)(
+                lambda make=make, both=both: (both(send_sem).wait() if both else make(every).wait_send())
+            )
 
     begin(1, ROWS, every, (HBM,))
     loads[0].wait()
     for t in range(tiles):
         for l in range(layers):
-            put_edges(et_y, l, t, ext_y[l, span(t, HALO), :])
+            put_edges(1, l, t, ext_y[l, span(t, HALO), :])
     put_corners(
         ct_y,
         [ext_y[l, span(0, HALO), :] for l in range(layers)],
         [ext_y[l, span(tiles - 1, HALO), :] for l in range(layers)],
     )
-    begin(1, SIDE + CORNER, every)
+    begin(1, SIDE + CORNER, every, whole=True)
 
     def lower_of(step):
-        return order[: tiles // 2]
+        return order[::2]
 
     def up(step, t):
         side = step % 2
@@ -339,18 +365,20 @@
         for l in range(layers):
             part[l, span(t), :] = area[l * TILE : (l + 1) * TILE]
 
-    def box_early(field, which, then=None):
+    def box_early(field, which):
         ext = (ext_u, ext_y)[field]
         for t in range(tiles):
             if t not in ends:
                 box_own(ext, which, t)
         arrived(field, ROWS)
-        if then is not None:
-            then()
         for t in ends:
             box_own(ext, which, t)
         arrived(field, CORNER + SIDE)
-        take_corners((ct_u, ct_y)[field], (ht_u, ht_y)[field])
+        ht, ex = ((ht_u, ex_u), (ht_y, ex_y))[field]
+        take_corners((ct_u, ct_y)[field], ht)
+        row = HALO - HALF if field == 0 else HALO + HALF - 1
+        for l in range(layers):
+            ht[l, row : row + 1, TILE : TILE + rows] = ex[1, l : l + 1]
 
     def box_late(ht, which, t):
         halo = ht[:, :, t * TILE : (t + 3) * TILE].reshape(width, 3 * TILE)
@@ -438,7 +466,7 @@
                     primal_sum = primal_sum + fold(moved)
                     value = new + moved + dens[at]
                     ext_u[l, span(t, HALO), :] = value
-                    put_edges(et_u, l, t, value)
+                    put_edges(0, l, t, value)
             first_layer = some_layers[0]
             some = pl.ds(first_layer, len(some_layers))
             corner_ready = 0 in some_layers and ends[-1] in some_tiles
@@ -448,11 +476,6 @@
                     [ext_u[l, span(0, HALO), :] for l in range(layers)],
                     [ext_u[l, span(tiles - 1, HALO), :] for l in range(layers)],
                 )
-            begin(0, SIDE, some, some_tiles)
-            if ends[-1] in some_tiles:
-                begin(0, ROWS, some)
-            if corner_ready:
-                begin(0, CORNER, every)
             if 0 in some_layers:
 
                 @pl.when(has_below)
@@ -469,6 +492,11 @@
                     for t in going:
                         up(step, t).start()
 
+            begin(0, SIDE, some, some_tiles, (some_layers, some_tiles) == blocks[-1])
+            if ends[-1] in some_tiles:
+                begin(0, ROWS, some)
+            if corner_ready:
+                begin(0, CORNER, every)
             if step == 0:
                 if (some_layers, some_tiles) == blocks[1]:
                     hear(1)
@@ -491,20 +519,21 @@
                 z[at] = new
                 dual_sum = dual_sum + fold(new - old)
 
-        def other_half(last=last, step=step, lower=lower, upper=upper):
+        def other_half(n, last=last, step=step, lower=lower, upper=upper):
             @pl.when(has_below)
             def _():
-                for t in upper:
+                for t in upper[n::2]:
                     down(step, t).start()
 
             if not last:
 
                 @pl.when(has_above)
                 def _():
-                    for t in lower:
+                    for t in lower[n::2]:
                         up(step, t).start()
 
-        box_early(0, 0, other_half)
+        box_early(0, 0)
+        other_half(0)
         if step == 0:
             hear(2)
         for t in order:
@@ -528,10 +557,10 @@
                     y_out[at] = new
                 else:
                     ext_y[l, span(t, HALO), :] = new
-                    put_edges(et_y, l, t, new)
+                    put_edges(1, l, t, new)
 
         if not last:
-            begin(1, SIDE, every, rest)
+            begin(1, SIDE, every, rest, True)
 
         def update_top(t, now=now, update=update):
             at = (top, span(t), slice(None))
@@ -566,6 +595,7 @@
             for n in range(3, rounds):
                 hear(n)
         sums_begin(step, primal_sum, dual_sum)
+        other_half(1)
 
         def finish(last=last, step=step, now=now, lower=lower, upper=upper, landed=landed,
                    update_top=update_top, update_low=update_low):
@@ -614,6 +644,7 @@
     et = pltpu.VMEM((layers, 2 * HALO, rows), F32)
     ht = pltpu.VMEM((layers, 2 * HALO, rows + 2 * TILE), F32)
     ct = pltpu.VMEM((2, 2, 2 * HALO, TILE), F32)
+    ex = pltpu.VMEM((2, layers, rows), F32)
     plane = pltpu.VMEM((rows, cols), F32)
     planes = pltpu.VMEM((2, rows, cols), F32)
     x, y, z, weight = pl.pallas_call(
@@ -623,7 +654,7 @@
         out_specs=(vmem,) * 4,
         scratch_shapes=[
             fields, field_flags,
-            ext, ext, et, et, ht, ht, ct, ct, planes, planes, plane, full, full, full,
+            ext, ext, et, et, ht, ht, ct, ct, ex, ex, planes, planes, plane, full, full, full,
             pltpu.VMEM((2, TILE, TILE + 2 * HALO), BF16),
             pltpu.VMEM((2, TILE, 3 * TILE), BF16),
             pltpu.VMEM((2, 2 * cols, cols), BF16),

time: 46 us -> 45 us (0.978)
  Pallas kernels: 44.1 us -> 43 us
    pallas_call x1, Pallas kernels: 42.9 us -> 41.8 us  [local(): pl.pallas_call(functools.partial(kernel, sizes), out_shape=(full, full, f...]
where the time goes in v3:
time: 45 us; the launch traced here: 44.8 us
  Pallas kernels  43 us (96%)
  between operations  1.81 us (4%)
    pallas_call x1, Pallas kernels, local(): pl.pallas_call(functools.partial(kernel, sizes), out_shape=(full, full, f...  41.8 us
    pallas_call x1, Pallas kernels, local(): pl.pallas_call(flush, out_shape=(whole,) * 3, in_specs=[anywhere] * 3, ou...  1.19 us

profile of v3, /device:TPU:0, one launch (start us, length us, event | category | flops | bytes accessed | tf_op | source)
XLA Modules:
  0.0 44.8 jit_solution(4730636967360973603)
XLA Ops:
  0.6 41.8 %fill_steps.1 = (f32[2,512,128]{2,1,0:T(8,128)S(1)}, f32[2,512,128]{2,1,0:T(8,128)S(1)}, f32[2,512,128]{2,1,0:T(8,128)S(1)}, f32[1,128]{1,0:T(1,128)S(1)}) custom-call(f32[2,512,128]{2,1,0:T(8,128)} %cost_in.1, f32[2,512,128]{2,1,0:T(8,128)} %dens_in.1, s32[2,512,128]{2,1,0:T(8,128)} %capc_in.1, s32[2,512,128]{2,1,0:T(8,128)} %blocked_in.1, ...), custom_call_target="tpu_custom_call" | custom-call | tf_op jit(solution)/shard_map/fill_steps/pallas_call | solution.py:650
  42.4 1.2 %flush.1 = (f32[2,512,128]{2,1,0:T(8,128)}, f32[2,512,128]{2,1,0:T(8,128)}, f32[2,512,128]{2,1,0:T(8,128)}) custom-call(f32[2,512,128]{2,1,0:T(8,128)S(1)} %get-tuple-element.11.refs_0_, f32[2,512,128]{2,1,0:T(8,128)S(1)} %get-tuple-element.12.refs_1_, f32[2,512,128]{2,1,0:T(8,128)S(1)} %get-tuple-element.13.refs_2_), custom_call_target="tpu_custom_call" | custom-call | tf_op jit(solution)/shard_map/flush/pallas_call | solution.py:677

commit v4 on v3

--- a/solution.py
+++ b/solution.py
@@ -87,8 +87,6 @@
         (y_in, ext_y.at[:, own, :], 0), (z_in, z, 1), (cost_in, cost, 2), (dens_in, dens, 2),
         (x_in, x, 3), (capc_in, capc, 4), (blocked_in, blocked, 4),
     )
-    for a, b, n in pairs:
-        pltpu.make_async_copy(a, b, load_sem.at[n]).start()
     loads = [
         pltpu.make_async_copy(ref, ref, load_sem.at[n])
         for n, ref in enumerate((ext_y.at[:, own, :], z, reals, x, flags))
@@ -97,7 +95,7 @@
     for ref in (ext_u, ext_y):
         ref[:, :HALO, :] = jnp.zeros((layers, HALO, cols), F32)
         ref[:, HALO + rows :, :] = jnp.zeros((layers, HALO, cols), F32)
-    for ref in (ht_u, ht_y, ct_u, ct_y, ex_u, ex_y, above, below, zlow):
+    for ref in (ht_u, ht_y, ct_u, ct_y, ex_u, ex_y):
         ref[...] = jnp.zeros(ref.shape, F32)
 
     barrier = pltpu.get_barrier_semaphore()
@@ -147,6 +145,17 @@
         pl.semaphore_wait(semaphore, sum(there.astype(jnp.int32) for there, _ in peers))
 
     signal_some(barrier, beside(1) + corners)
+    for a, b, n in pairs:
+        pltpu.make_async_copy(a, b, load_sem.at[n]).start()
+
+    @pl.when(jnp.logical_not(has_above))
+    def _():
+        above[...] = jnp.zeros(above.shape, F32)
+
+    @pl.when(jnp.logical_not(has_below))
+    def _():
+        below[...] = jnp.zeros(below.shape, F32)
+        zlow[...] = jnp.zeros(zlow.shape, F32)
 
     spread = spreads(sizes)
     rounds = len(spread) + 2
@@ -171,10 +180,12 @@
 
     def first_up(t):
         return pltpu.make_async_remote_copy(
-            src_ref=z_in.at[top, span(t), :], dst_ref=zlow.at[span(t), :],
+            src_ref=z.at[top, span(t), :], dst_ref=zlow.at[span(t), :],
             send_sem=first_sem.at[tiles], recv_sem=first_sem.at[t],
             device_id=(il + 1, ir, ic), device_id_type=MESH,
         )
+
+    loads[1].wait()
 
     @pl.when(has_above)
     def _():
@@ -313,14 +324,18 @@
     )
     begin(1, SIDE + CORNER, every, whole=True)
 
-    def lower_of(step):
-        return order[::2]
+    lower, upper = order[::2], order[1::2]
+
+    def portion(t, way):
+        if t in (upper, lower)[way]:
+            return 0
+        return 1 + (lower, upper)[way].index(t) % 2
 
     def up(step, t):
         side = step % 2
         return pltpu.make_async_remote_copy(
             src_ref=ext_u.at[top, span(t, HALO), :], dst_ref=below.at[side, span(t), :],
-            send_sem=zsend.at[side, 0], recv_sem=zrecv.at[side, 0, int(t in lower_of(step))],
+            send_sem=zsend.at[side, 0], recv_sem=zrecv.at[side, 0, portion(t, 0)],
             device_id=(il + 1, ir, ic), device_id_type=MESH,
         )
 
@@ -328,7 +343,7 @@
         side = step % 2
         return pltpu.make_async_remote_copy(
             src_ref=ext_u.at[0, span(t, HALO), :], dst_ref=above.at[side, span(t), :],
-            send_sem=zsend.at[side, 1], recv_sem=zrecv.at[side, 1, int(t not in lower_of(step))],
+            send_sem=zsend.at[side, 1], recv_sem=zrecv.at[side, 1, portion(t, 1)],
             device_id=(il - 1, ir, ic), device_id_type=MESH,
         )
 
@@ -354,25 +369,28 @@
                         halo_cols if m == l else blank
                     )
 
-    def box_own(ext, which, t):
-        tall = pl.ds(t * TILE, TILE + 2 * HALO)
-        wide = jnp.concatenate([ext[l, tall, :].astype(BF16) for l in range(layers)], axis=1)
-        mid = dot(band_r[which], wide)
-        pieces = [
-            jnp.concatenate(split(mid[:, l * cols : (l + 1) * cols]), axis=1) for l in range(layers)
-        ]
+    def box_own(ext, which, some_tiles):
+        pieces = []
+        for t in some_tiles:
+            tall = pl.ds(t * TILE, TILE + 2 * HALO)
+            wide = jnp.concatenate([ext[l, tall, :].astype(BF16) for l in range(layers)], axis=1)
+            mid = dot(band_r[which], wide)
+            pieces += [
+                jnp.concatenate(split(mid[:, l * cols : (l + 1) * cols]), axis=1)
+                for l in range(layers)
+            ]
         area = dot(jnp.concatenate(pieces, axis=0), inner[which])
-        for l in range(layers):
-            part[l, span(t), :] = area[l * TILE : (l + 1) * TILE]
+        for n, t in enumerate(some_tiles):
+            for l in range(layers):
+                at = (n * layers + l) * TILE
+                part[l, span(t), :] = area[at : at + TILE]
 
     def box_early(field, which):
         ext = (ext_u, ext_y)[field]
-        for t in range(tiles):
-            if t not in ends:
-                box_own(ext, which, t)
+        if rest:
+            box_own(ext, which, rest)
         arrived(field, ROWS)
-        for t in ends:
-            box_own(ext, which, t)
+        box_own(ext, which, ends)
         arrived(field, CORNER + SIDE)
         ht, ex = ((ht_u, ex_u), (ht_y, ex_y))[field]
         take_corners((ct_u, ct_y)[field], ht)
@@ -380,14 +398,24 @@
         for l in range(layers):
             ht[l, row : row + 1, TILE : TILE + rows] = ex[1, l : l + 1]
 
-    def box_late(ht, which, t):
-        halo = ht[:, :, t * TILE : (t + 3) * TILE].reshape(width, 3 * TILE)
+    def box_late(ht, which, some_tiles):
+        halo = jnp.concatenate(
+            [ht[:, :, t * TILE : (t + 3) * TILE].reshape(width, 3 * TILE) for t in some_tiles], axis=0
+        )
         side = dot(band_h[which], halo.astype(BF16), NT)
-        area = dot(jnp.concatenate(split(side), axis=1), outer[which])
-        return [part[l, span(t), :] + area[:, l * cols : (l + 1) * cols] for l in range(layers)]
-
-    loads[1].wait()
-    z[top] = z[top] * keep_top
+        sides = [side[:, n * width : (n + 1) * width] for n in range(len(some_tiles))]
+        area = dot(jnp.concatenate([jnp.concatenate(split(v), axis=1) for v in sides], axis=0), outer[which])
+        return {
+            (l, t): part[l, span(t), :] + area[n * TILE : (n + 1) * TILE, l * cols : (l + 1) * cols]
+            for n, t in enumerate(some_tiles)
+            for l in range(layers)
+        }
+
+
+    @pl.when(jnp.logical_not(has_above))
+    def _():
+        z[top] = jnp.zeros((rows, cols), F32)
+
     for load in loads[2:]:
         load.wait()
     everywhere = [(l, t, (l, span(t), slice(None))) for t in order for l in range(layers)]
@@ -423,25 +451,24 @@
         ratio = jnp.broadcast_to((dual + tiny_term) / (primal + tiny_term), (1, cols))
         return jnp.sqrt(weight) * jnp.sqrt(jnp.sqrt(ratio))
 
+    finish = None
     weight = jnp.ones((1, cols), F32)
     for step in range(ITERS):
         last = step == ITERS - 1
         now = step % 2
-        lower = lower_of(step)
-        upper = [t for t in order if t not in lower]
 
         box_early(1, 1)
-        for t in order:
-            for l, area in enumerate(box_late(ht_y, 1, t)):
-                at = (l, span(t), slice(None))
-                grad[at] = cost[at] + area * inverse_area
+        for (l, t), area in box_late(ht_y, 1, order).items():
+            at = (l, span(t), slice(None))
+            grad[at] = cost[at] + area * inverse_area
         if step > 0:
-            finish()
+            finish(0)
             weight = sums_end(step - 1, weight)
         tau = step_eta / weight
         sigma = step_eta * weight
         sigma_inverse = 1.0 / sigma
 
+        finish_before = finish
         primal_sum = jnp.zeros((8, cols), F32)
         groups = [g for g in (ends, rest) if g]
         if step == 0:
@@ -454,6 +481,8 @@
             if step == 0 and 0 in some_layers:
                 for t in some_tiles:
                     pl.when(has_below)(lambda t=t: first_up(t).wait_recv())
+            if step > 0 and (some_layers, some_tiles) == blocks[-1]:
+                finish_before(1)
             for t in some_tiles:
                 for l in some_layers:
                     at = (l, span(t), slice(None))
@@ -519,7 +548,7 @@
                 z[at] = new
                 dual_sum = dual_sum + fold(new - old)
 
-        def other_half(n, last=last, step=step, lower=lower, upper=upper):
+        def other_half(n, last=last, step=step):
             @pl.when(has_below)
             def _():
                 for t in upper[n::2]:
@@ -536,7 +565,12 @@
         other_half(0)
         if step == 0:
             hear(2)
+        areas = {}
         for t in order:
+            if t == ends[0]:
+                areas |= box_late(ht_u, 0, ends)
+            if rest and t == rest[0]:
+                areas |= box_late(ht_u, 0, rest)
             if not last and rest and t == rest[0]:
                 put_corners(
                     ct_y,
@@ -545,7 +579,8 @@
                 )
                 begin(1, SIDE, every, ends)
                 begin(1, ROWS + CORNER, every)
-            for l, area in enumerate(box_late(ht_u, 0, t)):
+            for l in range(layers):
+                area = areas[l, t]
                 at = (l, span(t), slice(None))
                 old = ext_y[l, span(t, HALO), :]
                 term = old * sigma_inverse + area * inverse_area
@@ -575,13 +610,13 @@
             zlow[span(t), :] = new
             return fold(new - old)
 
-        def landed(downs, ups, now=now, lower=lower):
+        def landed(downs, ups, now=now):
             for there, plane, way, some in (
                 (has_above, above, 1, downs), (has_below, below, 0, ups)
             ):
                 if some:
                     all_of = plane.at[now, pl.ds(0, len(some) * TILE), :]
-                    which = int((some == lower) == (way == 0))
+                    which = portion(some[0], way)
                     pl.when(there)(
                         pltpu.make_async_copy(all_of, all_of, zrecv.at[now, way, which]).wait
                     )
@@ -597,22 +632,24 @@
         sums_begin(step, primal_sum, dual_sum)
         other_half(1)
 
-        def finish(last=last, step=step, now=now, lower=lower, upper=upper, landed=landed,
+        def finish(n, last=last, step=step, now=now, landed=landed,
                    update_top=update_top, update_low=update_low):
-            landed(upper, [] if last else lower)
-            for t in upper:
+            if n == 0:
+                for there, way, gone in (
+                    (has_below, 1, order), (has_above, 0, upper if last else order)
+                ):
+                    all_of = above.at[now, pl.ds(0, len(gone) * TILE), :]
+                    pl.when(there)(pltpu.make_async_copy(all_of, all_of, zsend.at[now, way]).wait)
+                departed(0)
+            landed(upper[n::2], [] if last else lower[n::2])
+            for t in upper[n::2]:
                 update_top(t)
             if not last:
-                for t in lower:
+                for t in lower[n::2]:
                     update_low(t)
 
-            for there, way, gone in ((has_below, 1, order), (has_above, 0, upper if last else order)):
-                all_of = above.at[now, pl.ds(0, len(gone) * TILE), :]
-                pl.when(there)(pltpu.make_async_copy(all_of, all_of, zsend.at[now, way]).wait)
-
-            departed(0)
-
-    finish()
+    finish(0)
+    finish(1)
     weight_out[...] = sums_end(ITERS - 1, weight)
 
 
@@ -620,14 +657,15 @@
     count = len(refs) // 2
     ins, outs, sem = refs[:count], refs[count : 2 * count], refs[2 * count]
     moves = [
-        pltpu.make_async_copy(a.at[l], b.at[l], sem.at[n, l])
+        pltpu.make_async_copy(a.at[l, some], b.at[l, some], sem.at[n])
         for n, (a, b) in enumerate(zip(ins, outs))
         for l in range(a.shape[0])
+        for some in (pl.ds(0, a.shape[1] // 2), pl.ds(a.shape[1] // 2, a.shape[1] // 2))
     ]
     for move in moves:
         move.start()
-    for move in moves:
-        move.wait()
+    for n, (a, b) in enumerate(zip(ins, outs)):
+        pltpu.make_async_copy(a, b, sem.at[n]).wait()
 
 
 def local(sizes, *args):
@@ -666,7 +704,7 @@
             pltpu.SemaphoreType.DMA((2, 8)),
             pltpu.SemaphoreType.DMA((tiles + 1,)),
             pltpu.SemaphoreType.DMA((2, 2)),
-            pltpu.SemaphoreType.DMA((2, 2, 2)),
+            pltpu.SemaphoreType.DMA((2, 2, 3)),
             pltpu.SemaphoreType.DMA((2, ITERS)),
             pltpu.SemaphoreType.REGULAR((len(spreads(sizes)) + 2,)),
         ],
@@ -679,7 +717,7 @@
         out_shape=(whole,) * 3,
         in_specs=[anywhere] * 3,
         out_specs=(anywhere,) * 3,
-        scratch_shapes=[pltpu.SemaphoreType.DMA((3, layers))],
+        scratch_shapes=[pltpu.SemaphoreType.DMA((3,))],
         name="flush",
     )(*(pltpu.with_memory_space_constraint(value, pltpu.VMEM) for value in (x, y, z)))
     return x, y, z, weight[0, 0]

time: 45 us -> 44.5 us (0.989)
  no operation moved by 1% of the time
where the time goes in v4:
time: 44.5 us; the launch traced here: 44.4 us
  Pallas kernels  42.6 us (96%)
  between operations  1.81 us (4%)
    pallas_call x1, Pallas kernels, local(): pl.pallas_call(functools.partial(kernel, sizes), out_shape=(full, full, f...  41.4 us
    pallas_call x1, Pallas kernels, local(): pl.pallas_call(flush, out_shape=(whole,) * 3, in_specs=[anywhere] * 3, ou...  1.15 us

profile of v4, /device:TPU:0, one launch (start us, length us, event | category | flops | bytes accessed | tf_op | source)
XLA Modules:
  0.0 44.4 jit_solution(12145684281814101048)
XLA Ops:
  0.6 41.4 %fill_steps.1 = (f32[2,512,128]{2,1,0:T(8,128)S(1)}, f32[2,512,128]{2,1,0:T(8,128)S(1)}, f32[2,512,128]{2,1,0:T(8,128)S(1)}, f32[1,128]{1,0:T(1,128)S(1)}) custom-call(f32[2,512,128]{2,1,0:T(8,128)} %cost_in.1, f32[2,512,128]{2,1,0:T(8,128)} %dens_in.1, s32[2,512,128]{2,1,0:T(8,128)} %capc_in.1, s32[2,512,128]{2,1,0:T(8,128)} %blocked_in.1, ...), custom_call_target="tpu_custom_call" | custom-call | tf_op jit(solution)/shard_map/fill_steps/pallas_call | solution.py:688
  42.1 1.2 %flush.1 = (f32[2,512,128]{2,1,0:T(8,128)}, f32[2,512,128]{2,1,0:T(8,128)}, f32[2,512,128]{2,1,0:T(8,128)}) custom-call(f32[2,512,128]{2,1,0:T(8,128)S(1)} %get-tuple-element.11.refs_0_, f32[2,512,128]{2,1,0:T(8,128)S(1)} %get-tuple-element.12.refs_1_, f32[2,512,128]{2,1,0:T(8,128)S(1)} %get-tuple-element.13.refs_2_), custom_call_target="tpu_custom_call" | custom-call | tf_op jit(solution)/shard_map/flush/pallas_call | solution.py:715

commit v5 on v4

--- a/solution.py
+++ b/solution.py
@@ -427,15 +427,15 @@
         return jnp.sum((value * value).reshape(TILE // 8, 8, cols), axis=0)
 
     def sums_begin(step, primal_sum, dual_sum):
-        slots[step, pl.ds(me, 1)] = jnp.concatenate(
-            [jnp.sum(primal_sum, axis=0, keepdims=True), jnp.sum(dual_sum, axis=0, keepdims=True)],
-            axis=0,
-        )[None]
+        left = iota((8, cols), 1) < cols // 2
+        both = jnp.where(left, primal_sum, dual_sum)
+        across = pltpu.roll(jnp.where(left, dual_sum, primal_sum), cols // 2, axis=1)
+        slots[step, pl.ds(me, 1)] = jnp.sum(both + across, axis=0, keepdims=True)[None]
 
         def send(device):
             pltpu.make_async_remote_copy(
                 src_ref=slots.at[step, me], dst_ref=slots.at[step, me],
-                send_sem=sum_sem.at[0, step], recv_sem=sum_sem.at[1, step],
+                send_sem=sum_sem.at[ITERS], recv_sem=sum_sem.at[step],
                 device_id=device, device_id_type=MESH,
             ).start()
 
@@ -443,11 +443,11 @@
 
     def sums_end(step, weight):
         some = slots.at[step, pl.ds(0, ndev - 1)]
-        pltpu.make_async_copy(some, some, sum_sem.at[1, step]).wait()
-        pltpu.make_async_copy(some, some, sum_sem.at[0, step]).wait()
+        pltpu.make_async_copy(some, some, sum_sem.at[step]).wait()
         both = jnp.sum(slots[step], axis=0)
-        primal = jnp.sum(both[0:1], axis=1, keepdims=True)
-        dual = jnp.sum(both[1:2], axis=1, keepdims=True)
+        left = iota((1, cols), 1) < cols // 2
+        primal = jnp.sum(jnp.where(left, both, 0.0), axis=1, keepdims=True)
+        dual = jnp.sum(jnp.where(left, 0.0, both), axis=1, keepdims=True)
         ratio = jnp.broadcast_to((dual + tiny_term) / (primal + tiny_term), (1, cols))
         return jnp.sqrt(weight) * jnp.sqrt(jnp.sqrt(ratio))
 
@@ -470,7 +470,7 @@
 
         finish_before = finish
         primal_sum = jnp.zeros((8, cols), F32)
-        groups = [g for g in (ends, rest) if g]
+        groups = [g for g in (ends[:1], ends[1:], rest) if g]
         if step == 0:
             blocks = [(range(1, layers), g) for g in groups] + [(range(1), [t]) for t in order]
         else:
@@ -651,6 +651,8 @@
     finish(0)
     finish(1)
     weight_out[...] = sums_end(ITERS - 1, weight)
+    gone = slots.at[:, pl.ds(0, ndev - 1)]
+    pltpu.make_async_copy(gone, gone, sum_sem.at[ITERS]).wait()
 
 
 def flush(*refs):
@@ -698,14 +700,14 @@
             pltpu.VMEM((2, 2 * cols, cols), BF16),
             pltpu.VMEM((2, 2 * layers * 2 * HALO, layers * cols), BF16),
             pltpu.VMEM((2 * HALO, cols), BF16),
-            pltpu.VMEM((ITERS, ndev, 2, cols), F32),
+            pltpu.VMEM((ITERS, ndev, 1, cols), F32),
             pltpu.SemaphoreType.DMA((5,)),
             pltpu.SemaphoreType.DMA((2, 8)),
             pltpu.SemaphoreType.DMA((2, 8)),
             pltpu.SemaphoreType.DMA((tiles + 1,)),
             pltpu.SemaphoreType.DMA((2, 2)),
             pltpu.SemaphoreType.DMA((2, 2, 3)),
-            pltpu.SemaphoreType.DMA((2, ITERS)),
+            pltpu.SemaphoreType.DMA((ITERS + 1,)),
             pltpu.SemaphoreType.REGULAR((len(spreads(sizes)) + 2,)),
         ],
         compiler_params=pltpu.CompilerParams(collective_id=0, has_side_effects=True),

time: 44.5 us -> 44 us (0.989)
  Pallas kernels: 42.6 us -> 42.1 us
    pallas_call x1, Pallas kernels: 41.4 us -> 40.9 us  [local(): pl.pallas_call(functools.partial(kernel, sizes), out_shape=(full, full, f...]
where the time goes in v5:
time: 44 us; the launch traced here: 43.9 us
  Pallas kernels  42.1 us (96%)
  between operations  1.81 us (4%)
    pallas_call x1, Pallas kernels, local(): pl.pallas_call(functools.partial(kernel, sizes), out_shape=(full, full, f...  40.9 us
    pallas_call x1, Pallas kernels, local(): pl.pallas_call(flush, out_shape=(whole,) * 3, in_specs=[anywhere] * 3, ou...  1.15 us

profile of v5, /device:TPU:0, one launch (start us, length us, event | category | flops | bytes accessed | tf_op | source)
XLA Modules:
  0.0 43.9 jit_solution(15433314884104756807)
XLA Ops:
  0.6 40.9 %fill_steps.1 = (f32[2,512,128]{2,1,0:T(8,128)S(1)}, f32[2,512,128]{2,1,0:T(8,128)S(1)}, f32[2,512,128]{2,1,0:T(8,128)S(1)}, f32[1,128]{1,0:T(1,128)S(1)}) custom-call(f32[2,512,128]{2,1,0:T(8,128)} %cost_in.1, f32[2,512,128]{2,1,0:T(8,128)} %dens_in.1, s32[2,512,128]{2,1,0:T(8,128)} %capc_in.1, s32[2,512,128]{2,1,0:T(8,128)} %blocked_in.1, ...), custom_call_target="tpu_custom_call" | custom-call | tf_op jit(solution)/shard_map/fill_steps/pallas_call | solution.py:690
  41.6 1.2 %flush.1 = (f32[2,512,128]{2,1,0:T(8,128)}, f32[2,512,128]{2,1,0:T(8,128)}, f32[2,512,128]{2,1,0:T(8,128)}) custom-call(f32[2,512,128]{2,1,0:T(8,128)S(1)} %get-tuple-element.11.refs_0_, f32[2,512,128]{2,1,0:T(8,128)S(1)} %get-tuple-element.12.refs_1_, f32[2,512,128]{2,1,0:T(8,128)S(1)} %get-tuple-element.13.refs_2_), custom_call_target="tpu_custom_call" | custom-call | tf_op jit(solution)/shard_map/flush/pallas_call | solution.py:717

commit v6 on v5

--- a/solution.py
+++ b/solution.py
@@ -385,11 +385,15 @@
                 at = (n * layers + l) * TILE
                 part[l, span(t), :] = area[at : at + TILE]
 
-    def box_early(field, which):
+    def box_early(field, which, first=False):
         ext = (ext_u, ext_y)[field]
         if rest:
             box_own(ext, which, rest)
+        if first:
+            hear(0)
         arrived(field, ROWS)
+        if first:
+            hear(1)
         box_own(ext, which, ends)
         arrived(field, CORNER + SIDE)
         ht, ex = ((ht_u, ex_u), (ht_y, ex_y))[field]
@@ -457,7 +461,7 @@
         last = step == ITERS - 1
         now = step % 2
 
-        box_early(1, 1)
+        box_early(1, 1, step == 0)
         for (l, t), area in box_late(ht_y, 1, order).items():
             at = (l, span(t), slice(None))
             grad[at] = cost[at] + area * inverse_area
@@ -470,13 +474,11 @@
 
         finish_before = finish
         primal_sum = jnp.zeros((8, cols), F32)
-        groups = [g for g in (ends[:1], ends[1:], rest) if g]
+        groups = [g for g in (ends, rest) if g]
         if step == 0:
             blocks = [(range(1, layers), g) for g in groups] + [(range(1), [t]) for t in order]
         else:
             blocks = [(range(layers), g) for g in groups]
-        if step == 0:
-            hear(0)
         for some_layers, some_tiles in blocks:
             if step == 0 and 0 in some_layers:
                 for t in some_tiles:
@@ -527,8 +529,8 @@
             if corner_ready:
                 begin(0, CORNER, every)
             if step == 0:
-                if (some_layers, some_tiles) == blocks[1]:
-                    hear(1)
+                if (some_layers, some_tiles) == blocks[len(groups)]:
+                    hear(2)
         departed(1)
         if step == 0:
 
@@ -563,8 +565,6 @@
 
         box_early(0, 0)
         other_half(0)
-        if step == 0:
-            hear(2)
         areas = {}
         for t in order:
             if t == ends[0]:

time: 44 us -> 44 us (level)
  no operation moved by 1% of the time
where the time goes in v6:
time: 44 us; the launch traced here: 43.9 us
  Pallas kernels  42.1 us (96%)
  between operations  1.81 us (4%)
    pallas_call x1, Pallas kernels, local(): pl.pallas_call(functools.partial(kernel, sizes), out_shape=(full, full, f...  40.9 us
    pallas_call x1, Pallas kernels, local(): pl.pallas_call(flush, out_shape=(whole,) * 3, in_specs=[anywhere] * 3, ou...  1.15 us

profile of v6, /device:TPU:0, one launch (start us, length us, event | category | flops | bytes accessed | tf_op | source)
XLA Modules:
  0.0 43.9 jit_solution(1694275892514413110)
XLA Ops:
  0.6 40.9 %fill_steps.1 = (f32[2,512,128]{2,1,0:T(8,128)S(1)}, f32[2,512,128]{2,1,0:T(8,128)S(1)}, f32[2,512,128]{2,1,0:T(8,128)S(1)}, f32[1,128]{1,0:T(1,128)S(1)}) custom-call(f32[2,512,128]{2,1,0:T(8,128)} %cost_in.1, f32[2,512,128]{2,1,0:T(8,128)} %dens_in.1, s32[2,512,128]{2,1,0:T(8,128)} %capc_in.1, s32[2,512,128]{2,1,0:T(8,128)} %blocked_in.1, ...), custom_call_target="tpu_custom_call" | custom-call | tf_op jit(solution)/shard_map/fill_steps/pallas_call | solution.py:690
  41.6 1.2 %flush.1 = (f32[2,512,128]{2,1,0:T(8,128)}, f32[2,512,128]{2,1,0:T(8,128)}, f32[2,512,128]{2,1,0:T(8,128)}) custom-call(f32[2,512,128]{2,1,0:T(8,128)S(1)} %get-tuple-element.11.refs_0_, f32[2,512,128]{2,1,0:T(8,128)S(1)} %get-tuple-element.12.refs_1_, f32[2,512,128]{2,1,0:T(8,128)S(1)} %get-tuple-element.13.refs_2_), custom_call_target="tpu_custom_call" | custom-call | tf_op jit(solution)/shard_map/flush/pallas_call | solution.py:717

commit v7 on v6

--- a/solution.py
+++ b/solution.py
@@ -564,7 +564,8 @@
                         up(step, t).start()
 
         box_early(0, 0)
-        other_half(0)
+        if not last:
+            other_half(0)
         areas = {}
         for t in order:
             if t == ends[0]:
@@ -630,6 +631,8 @@
             for n in range(3, rounds):
                 hear(n)
         sums_begin(step, primal_sum, dual_sum)
+        if last:
+            other_half(0)
         other_half(1)
 
         def finish(n, last=last, step=step, now=now, landed=landed,

time: 44 us -> 43.8 us (level)
  no operation moved by 1% of the time
where the time goes in v7:
time: 43.8 us; the launch traced here: 43.7 us
  Pallas kernels  41.9 us (96%)
  between operations  1.81 us (4%)
    pallas_call x1, Pallas kernels, local(): pl.pallas_call(functools.partial(kernel, sizes), out_shape=(full, full, f...  40.7 us
    pallas_call x1, Pallas kernels, local(): pl.pallas_call(flush, out_shape=(whole,) * 3, in_specs=[anywhere] * 3, ou...  1.15 us

profile of v7, /device:TPU:0, one launch (start us, length us, event | category | flops | bytes accessed | tf_op | source)
XLA Modules:
  0.0 43.7 jit_solution(10095786353723090673)
XLA Ops:
  0.6 40.7 %fill_steps.1 = (f32[2,512,128]{2,1,0:T(8,128)S(1)}, f32[2,512,128]{2,1,0:T(8,128)S(1)}, f32[2,512,128]{2,1,0:T(8,128)S(1)}, f32[1,128]{1,0:T(1,128)S(1)}) custom-call(f32[2,512,128]{2,1,0:T(8,128)} %cost_in.1, f32[2,512,128]{2,1,0:T(8,128)} %dens_in.1, s32[2,512,128]{2,1,0:T(8,128)} %capc_in.1, s32[2,512,128]{2,1,0:T(8,128)} %blocked_in.1, ...), custom_call_target="tpu_custom_call" | custom-call | tf_op jit(solution)/shard_map/fill_steps/pallas_call | solution.py:693
  41.4 1.2 %flush.1 = (f32[2,512,128]{2,1,0:T(8,128)}, f32[2,512,128]{2,1,0:T(8,128)}, f32[2,512,128]{2,1,0:T(8,128)}) custom-call(f32[2,512,128]{2,1,0:T(8,128)S(1)} %get-tuple-element.11.refs_0_, f32[2,512,128]{2,1,0:T(8,128)S(1)} %get-tuple-element.12.refs_1_, f32[2,512,128]{2,1,0:T(8,128)S(1)} %get-tuple-element.13.refs_2_), custom_call_target="tpu_custom_call" | custom-call | tf_op jit(solution)/shard_map/flush/pallas_call | solution.py:720
